TPU v7x, 32 devices: a whole 2x2x4 slice. The times are simulated.
32 devices in a mesh: sec: 4 (over y, core), term: 8 (over z, x).
Axes of the slice: x: 2, y: 2, z: 4, core: 2. Of those that a mesh axis runs over, the one named last changes fastest.
Arguments:
- center: float32 [4, 2, 256, 256], P('sec'), may hold values from -6 to 6
- site_maps: float32 [16, 256, 256], P('sec'), may hold values from -1 to 2
- section_sites: int32 [4], P('sec'), may hold values from 1 to 4, 8 in all
- left_edge: float32 [48, 256, 256], P('term'), may hold values from -0.375 to 0.375
- right_edge: float32 [48, 256, 256], P('term'), may hold values from -0.375 to 0.375
- coefficients: float32 [48], replicated, may hold values from -0.875 to 0.875
- term_ids: int32 [48], P('term'), may hold values from 0 to 47, each once
- sector_mask: int32 [48, 2], replicated, may hold values 0 or 1
Outputs:
- evolved: float32 [4, 2, 256, 256], P('sec')
Inputs may be any that keep to these rules, and one draw needn't show every extreme that they name: `section_sites`: the sites of all sections sum to 8, and some section has exactly 4. `term_ids`: each of the 48 terms stands in exactly one slot.
All inputs are finite; a program needn't handle non-finite values. No bound on the sum of `section_sites` on one device may be relied on, other than what follows from the above.
Results may differ from a plain program's by a relative error of at most 0.0003.
Values sent between devices are 32-bit elements; how exact they have to be, the bound alone decides.
No kernel may reach another device: no remote copies, remote signals or barrier semaphores. Data moves between devices by JAX's collectives and lax.ppermute only.
A program may use at most 64 MiB of HBM per device.

v0:
```python
import functools

import jax
import jax.numpy as jnp
from jax import lax
from jax.sharding import PartitionSpec as P


ORDER = 4
TAYLOR_STEP = 0.3
PAIR = 2


def product(left, right):
    return jnp.dot(left, right, precision=lax.Precision.HIGH, preferred_element_type=jnp.float32)


def swap(value, axis, bit):
    pairs = [(i, i ^ bit) for i in range(lax.axis_size(axis))]
    return lax.ppermute(value, axis, pairs)


def section_product(slots, count):
    factors = [slots[i] for i in range(slots.shape[0])]
    starts = list(range(len(factors)))
    while len(factors) > 1:
        merged, merged_starts = [], []
        for i in range(0, len(factors), 2):
            if i + 1 == len(factors):
                merged.append(factors[i])
            else:
                both = product(factors[i], factors[i + 1])
                merged.append(jnp.where(starts[i + 1] < count, both, factors[i]))
            merged_starts.append(starts[i])
        factors, starts = merged, merged_starts
    return factors[0]


def scan_maps(section_map):
    position = lax.axis_index("sec")
    sections = lax.axis_size("sec")
    segment = section_map
    identity = jnp.eye(section_map.shape[0], dtype=jnp.float32)
    prefix = suffix = identity
    bit = 1
    while bit < sections:
        other = swap(segment, "sec", bit)
        upper = (position & bit) != 0
        if bit == 1:
            prefix = jnp.where(upper, other, identity)
            suffix = jnp.where(upper, identity, other)
        else:
            grown = product(jnp.where(upper, other, suffix), jnp.where(upper, prefix, other))
            prefix = jnp.where(upper, grown, prefix)
            suffix = jnp.where(upper, suffix, grown)
        if 2 * bit < sections:
            segment = product(
                jnp.where(upper, other, segment), jnp.where(upper, segment, other)
            )
        bit *= 2
    return prefix, suffix


def reduce_chunks(partial, group, groups):
    chunks = partial.reshape(groups, partial.shape[0] // groups, partial.shape[1])
    pick = functools.partial(lax.dynamic_index_in_dim, chunks, axis=0, keepdims=False)
    arrived = [swap(pick(group ^ d), "term", PAIR * d) for d in range(1, groups)]
    return sum(arrived, pick(group))


def gather_chunks(chunk, group, groups):
    arrived = [swap(chunk, "term", PAIR * d) for d in range(1, groups)]
    whole = jnp.zeros((groups,) + chunk.shape, chunk.dtype)
    whole = lax.dynamic_update_index_in_dim(whole, chunk, group, 0)
    for d in range(1, groups):
        whole = lax.dynamic_update_index_in_dim(whole, arrived[d - 1], group ^ d, 0)
    return whole.reshape(groups * chunk.shape[0], chunk.shape[1])


def apply_terms(tensor, lefts, rights):
    terms, width = lefts.shape[0], tensor.shape[0]
    lefted = product(lefts.reshape(terms * width, width), tensor).reshape(terms, width, width)
    return jnp.einsum(
        "tik,tkl->il", lefted, rights, precision=lax.Precision.HIGH,
        preferred_element_type=jnp.float32,
    )


def on_device(
    center, site_maps, section_sites, left_edge, right_edge, coefficients, term_ids, sector_mask
):
    width = center.shape[2]
    slots = left_edge.shape[0]
    half = slots // 2
    groups = lax.axis_size("term") // PAIR
    place = lax.axis_index("term")
    group, mine = place // PAIR, place % PAIR
    spot = lax.axis_index("sec")
    core, side = spot & 1, (spot >> 1) & 1

    chosen = term_ids[:, None] == jnp.arange(coefficients.shape[0], dtype=jnp.int32)[None, :]
    slot_weight = jnp.sum(jnp.where(chosen, coefficients[None, :], 0.0), axis=1)
    slot_mask = jnp.sum(
        jnp.where(chosen[:, :, None], sector_mask.astype(jnp.float32)[None], 0.0), axis=1
    )
    weight = slot_weight[:, None] * slot_mask

    quarter = jnp.where(
        core == 0,
        lax.dynamic_slice_in_dim(left_edge, side * half, half, 0),
        lax.dynamic_slice_in_dim(right_edge, side * half, half, 0),
    ).reshape(2, half * width // 2, width)
    pieces = [swap(quarter[i], "term", 1) for i in range(2)]
    shared = [swap(pieces[i], "sec", 2) for i in range(2)]
    halves = jnp.concatenate(pieces + shared, axis=0).reshape(slots, width, width)
    traded = swap(halves, "sec", 1)
    for_mine = jnp.where(mine == 0, weight[:, 0], weight[:, 1])
    others = swap(jnp.where(mine == 0, weight[:, 1], weight[:, 0]), "term", 1)
    others = jnp.where(side == 0, others, jnp.roll(others, half))
    other_left = jnp.where(core == 0, halves, traded) * others[:, None, None]
    other_right = jnp.where(core == 0, traded, halves)

    section_map = section_product(site_maps, section_sites[0])
    prefix, suffix = scan_maps(section_map)

    base = center[0]
    turned = product(jnp.einsum("ij,sjk->sik", prefix, base, precision=lax.Precision.HIGH)
                     .reshape(PAIR * width, width), suffix).reshape(PAIR, width, width)

    lefted = jnp.einsum("tij,sjk->tsik", left_edge, turned, precision=lax.Precision.HIGH)
    lefted = lefted * weight[:, :, None, None]
    partial = jnp.einsum("tsik,tkl->sil", lefted, right_edge, precision=lax.Precision.HIGH)
    keep = lax.dynamic_index_in_dim(partial, mine, 0, keepdims=False)
    give = lax.dynamic_index_in_dim(partial, 1 - mine, 0, keepdims=False)
    partial = keep + swap(give, "term", 1)
    current = gather_chunks(reduce_chunks(partial, group, groups) * (-TAYLOR_STEP), group, groups)
    total = current

    gram_left = jnp.einsum("ij,kj->ik", prefix, prefix, precision=lax.Precision.HIGH)
    gram_right = jnp.einsum("ji,jk->ik", suffix, suffix, precision=lax.Precision.HIGH)
    lefts = jnp.concatenate([left_edge * for_mine[:, None, None], other_left], axis=0)
    rights = jnp.concatenate([right_edge, other_right], axis=0)
    lefts = product(lefts.reshape(-1, width), gram_left).reshape(lefts.shape)
    rights = jnp.einsum("ij,tjk->tik", gram_right, rights, precision=lax.Precision.HIGH)
    lefts_out = jnp.einsum("ji,tjk->tik", prefix, lefts, precision=lax.Precision.HIGH)
    rights_out = jnp.einsum("tij,kj->tik", rights, suffix, precision=lax.Precision.HIGH)

    for order in range(2, ORDER):
        partial = apply_terms(current, lefts, rights)
        current = reduce_chunks(partial, group, groups) * (-TAYLOR_STEP / order)
        current = gather_chunks(current, group, groups)
        total = total + current

    partial = apply_terms(current, lefts_out, rights_out)
    start = lax.dynamic_index_in_dim(base, mine, 0, keepdims=False)
    back = product(jnp.einsum("ji,jk->ik", prefix, total, precision=lax.Precision.HIGH), suffix.T)
    so_far = (start + back).reshape(groups, width // groups, width)
    chunk = reduce_chunks(partial, group, groups) * (-TAYLOR_STEP / ORDER)
    chunk = chunk + lax.dynamic_index_in_dim(so_far, group, 0, keepdims=False)
    other_chunk = swap(chunk, "term", 1)
    ours = gather_chunks(chunk, group, groups)
    theirs = gather_chunks(other_chunk, group, groups)
    evolved = jnp.stack(
        [jnp.where(mine == 0, ours, theirs), jnp.where(mine == 0, theirs, ours)]
    )
    return evolved[None]


def solution(mesh):
    in_specs = (
        P("sec", None, None, None),
        P("sec", None, None),
        P("sec"),
        P("term", None, None),
        P("term", None, None),
        P(),
        P("term"),
        P(),
    )
    out_specs = P("sec", None, None, None)
    return jax.shard_map(
        on_device, mesh=mesh, in_specs=in_specs, out_specs=out_specs, check_vma=False
    )
```

profile of v0, /device:TPU:0, one launch (start us, length us, event | category | flops | bytes accessed | tf_op | source)
XLA Modules:
  0.0 146.7 jit_solution(6641766132853473807)
XLA Ops:
  2.0 1.4 convolution_select_fusion.2
  6.9 2.6 %collective-permute-start.5 = (f32[6]{0:T(128)S(1)}, f32[6]{0:T(128)S(1)}, u32[]{:S(2)}, u32[]{:S(2)}) collective-permute-start(f32[6]{0:T(128)S(1)} %get-tuple-element.6), channel_id=1, source_target_pairs={{0,1},{1,0},{2,3},{3,2},{4,5},{5,4},{6,7},{7,6},{8,9},{9,8},{10,11... | collective-permute-start | bytes 80 | tf_op jit(solution)/shard_map/ppermute | solution.py:20
  9.6 1.5 %dynamic-slice_select_fusion = f32[3,256,256]{2,1,0:T(8,128)S(1)} fusion(f32[6,256,256]{2,1,0:T(8,128)} %param.12, s32[]{:T(128)S(6)} %select_n.222, f32[6,256,256]{2,1,0:T(8,128)} %param.11, pred[]{:T(512)S(6)} %eq.42), kind=kLoop, calls=%fused_computation.33 | loop fusion | flops 196608 | bytes 2359301 | tf_op jit(solution)/shard_map/jit(_where)/select_n | solution.py:108
  12.0 2.0 %collective-permute-start.1 = (f32[384,256]{1,0:T(8,128)}, f32[384,256]{1,0:T(8,128)}, u32[]{:S(2)}, u32[]{:S(2)}) collective-permute-start(f32[384,256]{1,0:T(8,128)} %get-tuple-element.18), channel_id=1, source_target_pairs={{0,1},{1,0},{2,3},{3,2},{4,5},{5,4},{6,7},{7,6},{8,9},{9,8},{10,11... | collective-permute-start | bytes 1179656 | tf_op jit(solution)/shard_map/ppermute | solution.py:20
  15.0 1.5 %collective-permute-start.7 = (f32[256,256]{1,0:T(8,128)}, f32[256,256]{1,0:T(8,128)}, u32[]{:S(2)}, u32[]{:S(2)}) collective-permute-start(f32[256,256]{1,0:T(8,128)} %fusion.37), channel_id=1, source_target_pairs={{0,16},{8,24},{16,0},{24,8},{1,17},{9,25},{17,1},{25,9},{2,18},{10... | collective-permute-start | bytes 786440 | tf_op jit(solution)/shard_map/ppermute | solution.py:20
  16.9 7.4 %collective-permute-done = f32[384,256]{1,0:T(8,128)} collective-permute-done((f32[384,256]{1,0:T(8,128)}, f32[384,256]{1,0:T(8,128)}, u32[]{:S(2)}, u32[]{:S(2)}) %collective-permute-start) | collective-permute-done | bytes 393248 | tf_op jit(solution)/shard_map/ppermute | solution.py:20
  24.3 1.5 %collective-permute-start.2 = (f32[384,256]{1,0:T(8,128)}, f32[384,256]{1,0:T(8,128)S(1)}, u32[]{:S(2)}, u32[]{:S(2)}) collective-permute-start(f32[384,256]{1,0:T(8,128)} %collective-permute-done), channel_id=1, source_target_pairs={{0,16},{8,24},{16,0},{24,8},{1,17},{9,25},{17,1},{25,9},{2,18},{10... | collective-permute-start | bytes 1179656 | tf_op jit(solution)/shard_map/ppermute | solution.py:20
  25.8 6.1 %collective-permute-done.1 = f32[384,256]{1,0:T(8,128)} collective-permute-done((f32[384,256]{1,0:T(8,128)}, f32[384,256]{1,0:T(8,128)}, u32[]{:S(2)}, u32[]{:S(2)}) %collective-permute-start.1) | collective-permute-done | bytes 393248 | tf_op jit(solution)/shard_map/ppermute | solution.py:20
  31.8 1.5 %collective-permute-start.3 = (f32[384,256]{1,0:T(8,128)}, f32[384,256]{1,0:T(8,128)S(1)}, u32[]{:S(2)}, u32[]{:S(2)}) collective-permute-start(f32[384,256]{1,0:T(8,128)} %collective-permute-done.1), channel_id=1, source_target_pairs={{0,16},{8,24},{16,0},{24,8},{1,17},{9,25},{17,1},{25,9},{2,18},{10... | collective-permute-start | bytes 1179656 | tf_op jit(solution)/shard_map/ppermute | solution.py:20
  34.6 1.4 convolution_bitcast_fusion.1
  36.5 1.5 %fusion.18 = f32[2,256,6,256]{3,1,2,0:T(8,128)S(1)} fusion(f32[2,256,256,1]{1,2,3,0:T(8,128)S(1)} %convolution_bitcast_fusion, f32[6,256,256]{2,1,0:T(8,128)S(1)} %copy-done), kind=kOutput, calls=%fused_computation.20 | convolution fusion | flops 1207959552 | bytes 5242880 | tf_op jit(solution)/shard_map/tij,sjk->tsik/dot_general | solution.py:130
  38.0 2.8 %fusion.21 = f32[2,256,256]{2,1,0:T(8,128)S(1)} fusion(f32[6,256,256]{2,1,0:T(8,128)S(1)} %copy-done.1, f32[2,256,6,256]{3,1,2,0:T(8,128)S(1)} %fusion.18, f32[6,2]{0,1:T(2,128)S(1)} %copy.19), kind=kOutput, calls=%fused_computation.24 | convolution fusion | flops 1208745984 | bytes 5242928 | tf_op jit(solution)/shard_map/tsik,tkl->sil/dot_general | solution.py:132
  43.7 4.4 %collective-permute-done.8 = f32[256,256]{1,0:T(8,128)S(1)} collective-permute-done((f32[256,256]{1,0:T(8,128)S(1)}, f32[256,256]{1,0:T(8,128)S(1)}, u32[]{:S(2)}, u32[]{:S(2)}) %collective-permute-start.8) | collective-permute-done | bytes 262176 | tf_op jit(solution)/shard_map/ppermute | solution.py:20
  48.2 2.7 %collective-permute-start.10 = (f32[64,256]{1,0:T(8,128)S(1)}, f32[64,256]{1,0:T(8,128)S(1)}, u32[]{:S(2)}, u32[]{:S(2)}) collective-permute-start(f32[64,256]{1,0:T(8,128)S(1)} %get-tuple-element.34), channel_id=1, source_target_pairs={{0,4},{1,5},{2,6},{3,7},{4,0},{5,1},{6,2},{7,3},{8,12},{9,13},{10,... | collective-permute-start | bytes 196616 | tf_op jit(solution)/shard_map/ppermute | solution.py:20
  52.7 2.3 %collective-permute-done.10 = f32[64,256]{1,0:T(8,128)S(1)} collective-permute-done((f32[64,256]{1,0:T(8,128)S(1)}, f32[64,256]{1,0:T(8,128)S(1)}, u32[]{:S(2)}, u32[]{:S(2)}) %collective-permute-start.10) | collective-permute-done | bytes 65568 | tf_op jit(solution)/shard_map/ppermute | solution.py:20
  55.0 1.9 %collective-permute-done.11 = f32[64,256]{1,0:T(8,128)S(1)} collective-permute-done((f32[64,256]{1,0:T(8,128)S(1)}, f32[64,256]{1,0:T(8,128)S(1)}, u32[]{:S(2)}, u32[]{:S(2)}) %collective-permute-start.11) | collective-permute-done | bytes 65568 | tf_op jit(solution)/shard_map/ppermute | solution.py:20
  57.8 2.7 %collective-permute-start.13 = (f32[64,256]{1,0:T(8,128)S(1)}, f32[64,256]{1,0:T(8,128)S(1)}, u32[]{:S(2)}, u32[]{:S(2)}) collective-permute-start(f32[64,256]{1,0:T(8,128)S(1)} %get-tuple-element.14), channel_id=1, source_target_pairs={{0,4},{1,5},{2,6},{3,7},{4,0},{5,1},{6,2},{7,3},{8,12},{9,13},{10,... | collective-permute-start | bytes 196616 | tf_op jit(solution)/shard_map/ppermute | solution.py:20
  60.5 1.7 %collective-permute-start.14 = (f32[64,256]{1,0:T(8,128)S(1)}, f32[64,256]{1,0:T(8,128)S(1)}, u32[]{:S(2)}, u32[]{:S(2)}) collective-permute-start(f32[64,256]{1,0:T(8,128)S(1)} %get-tuple-element.14), channel_id=1, source_target_pairs={{0,6},{1,7},{2,4},{3,5},{4,2},{5,3},{6,0},{7,1},{8,14},{9,15},{10,... | collective-permute-start | bytes 196616 | tf_op jit(solution)/shard_map/ppermute | solution.py:20
  63.1 3.5 %collective-permute-done.14 = f32[64,256]{1,0:T(8,128)S(1)} collective-permute-done((f32[64,256]{1,0:T(8,128)S(1)}, f32[64,256]{1,0:T(8,128)S(1)}, u32[]{:S(2)}, u32[]{:S(2)}) %collective-permute-start.14) | collective-permute-done | bytes 65568 | tf_op jit(solution)/shard_map/ppermute | solution.py:20
  67.0 1.5 %fusion = f32[12,256,256]{2,1,0:T(8,128)S(1)} fusion(f32[256,256,1]{1,0,2:T(8,128)S(1)} %convolution_bitcast_fusion.3, f32[6,256,256]{2,1,0:T(8,128)S(1)} %get-tuple-element.16, f32[6,256,256]{2,1,0:T(8,128)S(1)} %broadcast_multiply_fusion), kind=kOutput, calls=%fused_computation | convolution fusion | flops 1208745984 | bytes 6553600 | tf_op jit(solution)/shard_map/dot_general | solution.py:15
  68.5 1.5 %fusion.67 = f32[12,256,256]{2,1,0:T(8,128)S(1)} fusion(f32[12,256,256]{2,1,0:T(8,128)S(1)} %fusion, f32[256,256,1]{1,0,2:T(8,128)S(1)} %bitcast.237), kind=kOutput, calls=%fused_computation.132 | convolution fusion | flops 1207959552 | bytes 6553600 | tf_op jit(solution)/shard_map/dot_general | solution.py:15
  70.0 2.9 %fusion.4 = f32[12,256,256]{2,1,0:T(8,128)S(1)} fusion(f32[256,256,1]{1,0,2:T(8,128)S(1)} %convolution_bitcast_fusion.2, f32[6,256,256]{2,1,0:T(8,128)S(1)} %get-tuple-element.15, f32[6,256,256]{2,1,0:T(8,128)S(1)} %copy-done.1), kind=kOutput, calls=%fused_computation.4 | convolution fusion | flops 1208745984 | bytes 6553600 | tf_op jit(solution)/shard_map/ij,tjk->tik/dot_general | solution.py:144
  72.9 1.7 %fusion.12 = f32[256,256,1]{1,0,2:T(8,128)S(1)} fusion(f32[12,256,256]{2,1,0:T(8,128)S(1)} %fusion.67, f32[12,256,256]{2,1,0:T(8,128)S(1)} %fusion.4), kind=kOutput, calls=%fused_computation.12 | convolution fusion | flops 1207959552 | bytes 6553600 | tf_op jit(solution)/shard_map/tik,tkl->il/dot_general | solution.py:83
  74.8 2.3 %collective-permute-start.16 = (f32[64,256]{1,0:T(8,128)S(1)}, f32[64,256]{1,0:T(8,128)S(1)}, u32[]{:S(2)}, u32[]{:S(2)}) collective-permute-start(f32[64,256]{1,0:T(8,128)S(1)} %get-tuple-element.31), channel_id=1, source_target_pairs={{0,4},{1,5},{2,6},{3,7},{4,0},{5,1},{6,2},{7,3},{8,12},{9,13},{10,... | collective-permute-start | bytes 196616 | tf_op jit(solution)/shard_map/ppermute | solution.py:20
  77.0 2.1 %collective-permute-start.17 = (f32[64,256]{1,0:T(8,128)S(1)}, f32[64,256]{1,0:T(8,128)S(1)}, u32[]{:S(2)}, u32[]{:S(2)}) collective-permute-start(f32[64,256]{1,0:T(8,128)S(1)} %get-tuple-element.30), channel_id=1, source_target_pairs={{0,6},{1,7},{2,4},{3,5},{4,2},{5,3},{6,0},{7,1},{8,14},{9,15},{10,... | collective-permute-start | bytes 196616 | tf_op jit(solution)/shard_map/ppermute | solution.py:20
  80.0 3.7 %collective-permute-done.17 = f32[64,256]{1,0:T(8,128)S(1)} collective-permute-done((f32[64,256]{1,0:T(8,128)S(1)}, f32[64,256]{1,0:T(8,128)S(1)}, u32[]{:S(2)}, u32[]{:S(2)}) %collective-permute-start.17) | collective-permute-done | bytes 65568 | tf_op jit(solution)/shard_map/ppermute | solution.py:20
  83.8 2.1 %collective-permute-start.19 = (f32[64,256]{1,0:T(8,128)S(1)}, f32[64,256]{1,0:T(8,128)S(1)}, u32[]{:S(2)}, u32[]{:S(2)}) collective-permute-start(f32[64,256]{1,0:T(8,128)S(1)} %get-tuple-element.12), channel_id=1, source_target_pairs={{0,4},{1,5},{2,6},{3,7},{4,0},{5,1},{6,2},{7,3},{8,12},{9,13},{10,... | collective-permute-start | bytes 196616 | tf_op jit(solution)/shard_map/ppermute | solution.py:20
  85.9 2.3 %collective-permute-start.20 = (f32[64,256]{1,0:T(8,128)S(1)}, f32[64,256]{1,0:T(8,128)S(1)}, u32[]{:S(2)}, u32[]{:S(2)}) collective-permute-start(f32[64,256]{1,0:T(8,128)S(1)} %get-tuple-element.12), channel_id=1, source_target_pairs={{0,6},{1,7},{2,4},{3,5},{4,2},{5,3},{6,0},{7,1},{8,14},{9,15},{10,... | collective-permute-start | bytes 196616 | tf_op jit(solution)/shard_map/ppermute | solution.py:20
  89.0 3.5 %collective-permute-done.20 = f32[64,256]{1,0:T(8,128)S(1)} collective-permute-done((f32[64,256]{1,0:T(8,128)S(1)}, f32[64,256]{1,0:T(8,128)S(1)}, u32[]{:S(2)}, u32[]{:S(2)}) %collective-permute-start.20) | collective-permute-done | bytes 65568 | tf_op jit(solution)/shard_map/ppermute | solution.py:20
  92.5 1.5 %fusion.68 = f32[12,256,256]{2,1,0:T(8,128)S(1)} fusion(f32[12,256,256]{2,1,0:T(8,128)S(1)} %fusion, f32[256,256,1]{1,0,2:T(8,128)S(1)} %bitcast.238), kind=kOutput, calls=%fused_computation.133 | convolution fusion | flops 1207959552 | bytes 6553600 | tf_op jit(solution)/shard_map/dot_general | solution.py:15
  94.0 1.7 %fusion.10 = f32[256,256,1]{1,0,2:T(8,128)S(1)} fusion(f32[12,256,256]{2,1,0:T(8,128)S(1)} %fusion.68, f32[12,256,256]{2,1,0:T(8,128)S(1)} %fusion.4), kind=kOutput, calls=%fused_computation.10 | convolution fusion | flops 1207959552 | bytes 6553600 | tf_op jit(solution)/shard_map/tik,tkl->il/dot_general | solution.py:83
  95.8 3.0 %collective-permute-start.22 = (f32[64,256]{1,0:T(8,128)S(1)}, f32[64,256]{1,0:T(8,128)S(1)}, u32[]{:S(2)}, u32[]{:S(2)}) collective-permute-start(f32[64,256]{1,0:T(8,128)S(1)} %get-tuple-element.28), channel_id=1, source_target_pairs={{0,4},{1,5},{2,6},{3,7},{4,0},{5,1},{6,2},{7,3},{8,12},{9,13},{10,... | collective-permute-start | bytes 196616 | tf_op jit(solution)/shard_map/ppermute | solution.py:20
  98.8 1.4 collective-permute-start.23
  100.2 2.7 %fusion.28 = f32[12,256,256]{2,1,0:T(8,128)S(1)} fusion(f32[12,256,256]{2,1,0:T(8,128)S(1)} %fusion, f32[256,256]{1,0:T(8,128)S(1)} %get-tuple-element.22), kind=kOutput, calls=%fused_computation.48 | convolution fusion | flops 1207959552 | bytes 6553600 | tf_op jit(solution)/shard_map/ji,tjk->tik/dot_general | solution.py:145
  103.0 2.5 %collective-permute-done.23 = f32[64,256]{1,0:T(8,128)S(1)} collective-permute-done((f32[64,256]{1,0:T(8,128)S(1)}, f32[64,256]{1,0:T(8,128)S(1)}, u32[]{:S(2)}, u32[]{:S(2)}) %collective-permute-start.23) | collective-permute-done | bytes 65568 | tf_op jit(solution)/shard_map/ppermute | solution.py:20
  106.7 2.9 %fusion.8 = f32[12,256,256]{2,1,0:T(8,128)S(1)} fusion(f32[12,256,256]{2,1,0:T(8,128)S(1)} %fusion.4, f32[256,256]{1,0:T(8,128)S(1)} %get-tuple-element.21), kind=kOutput, calls=%fused_computation.8 | convolution fusion | flops 1207959552 | bytes 6553600 | tf_op jit(solution)/shard_map/tij,kj->tik/dot_general | solution.py:146
  110.4 2.5 %collective-permute-start.26 = (f32[64,256]{1,0:T(8,128)S(1)}, f32[64,256]{1,0:T(8,128)S(1)}, u32[]{:S(2)}, u32[]{:S(2)}) collective-permute-start(f32[64,256]{1,0:T(8,128)S(1)} %get-tuple-element.10), channel_id=1, source_target_pairs={{0,6},{1,7},{2,4},{3,5},{4,2},{5,3},{6,0},{7,1},{8,14},{9,15},{10,... | collective-permute-start | bytes 196616 | tf_op jit(solution)/shard_map/ppermute | solution.py:20
  112.9 5.0 %collective-permute-done.25 = f32[64,256]{1,0:T(8,128)S(1)} collective-permute-done((f32[64,256]{1,0:T(8,128)S(1)}, f32[64,256]{1,0:T(8,128)S(1)}, u32[]{:S(2)}, u32[]{:S(2)}) %collective-permute-start.25) | collective-permute-done | bytes 65568 | tf_op jit(solution)/shard_map/ppermute | solution.py:20
  118.0 2.8 %fusion.15 = f32[12,256,256]{2,1,0:T(8,128)S(1)} fusion(f32[256,256,1]{1,0,2:T(8,128)S(1)} %bitcast.239, f32[12,256,256]{2,1,0:T(8,128)S(1)} %fusion.28), kind=kOutput, calls=%fused_computation.16 | convolution fusion | flops 1207959552 | bytes 6553600 | tf_op jit(solution)/shard_map/dot_general | solution.py:15
  120.8 1.7 %fusion.69 = f32[256,256,1]{1,0,2:T(8,128)S(1)} fusion(f32[12,256,256]{2,1,0:T(8,128)S(1)} %fusion.15, f32[12,256,256]{2,1,0:T(8,128)S(1)} %fusion.8), kind=kOutput, calls=%fused_computation.134 | convolution fusion | flops 1207959552 | bytes 6553600 | tf_op jit(solution)/shard_map/tik,tkl->il/dot_general | solution.py:83
  122.5 2.0 %collective-permute-start.27 = (f32[64,256]{1,0:T(8,128)S(1)}, f32[64,256]{1,0:T(8,128)S(1)}, u32[]{:S(2)}, u32[]{:S(2)}) collective-permute-start(f32[64,256]{1,0:T(8,128)S(1)} %get-tuple-element.23), channel_id=1, source_target_pairs={{0,2},{1,3},{2,0},{3,1},{4,6},{5,7},{6,4},{7,5},{8,10},{9,11},{10,... | collective-permute-start | bytes 196616 | tf_op jit(solution)/shard_map/ppermute | solution.py:20
  124.6 2.4 %collective-permute-start.29 = (f32[64,256]{1,0:T(8,128)S(1)}, f32[64,256]{1,0:T(8,128)S(1)}, u32[]{:S(2)}, u32[]{:S(2)}) collective-permute-start(f32[64,256]{1,0:T(8,128)S(1)} %get-tuple-element.24), channel_id=1, source_target_pairs={{0,6},{1,7},{2,4},{3,5},{4,2},{5,3},{6,0},{7,1},{8,14},{9,15},{10,... | collective-permute-start | bytes 196616 | tf_op jit(solution)/shard_map/ppermute | solution.py:20
  128.0 3.6 %collective-permute-done.28 = f32[64,256]{1,0:T(8,128)S(1)} collective-permute-done((f32[64,256]{1,0:T(8,128)S(1)}, f32[64,256]{1,0:T(8,128)S(1)}, u32[]{:S(2)}, u32[]{:S(2)}) %collective-permute-start.28) | collective-permute-done | bytes 65568 | tf_op jit(solution)/shard_map/ppermute | solution.py:20
  131.6 1.5 %collective-permute-start.33 = (f32[64,256]{1,0:T(8,128)S(1)}, f32[64,256]{1,0:T(8,128)S(1)}, u32[]{:S(2)}, u32[]{:S(2)}) collective-permute-start(f32[64,256]{1,0:T(8,128)S(1)} %get-tuple-element.8), channel_id=1, source_target_pairs={{0,1},{1,0},{2,3},{3,2},{4,5},{5,4},{6,7},{7,6},{8,9},{9,8},{10,11... | collective-permute-start | bytes 196616 | tf_op jit(solution)/shard_map/ppermute | solution.py:20
  135.2 2.3 %collective-permute-start.32 = (f32[64,256]{1,0:T(8,128)S(1)}, f32[64,256]{1,0:T(8,128)S(1)}, u32[]{:S(2)}, u32[]{:S(2)}) collective-permute-start(f32[64,256]{1,0:T(8,128)S(1)} %get-tuple-element.8), channel_id=1, source_target_pairs={{0,6},{1,7},{2,4},{3,5},{4,2},{5,3},{6,0},{7,1},{8,14},{9,15},{10,... | collective-permute-start | bytes 196616 | tf_op jit(solution)/shard_map/ppermute | solution.py:20
  137.8 1.8 %collective-permute-start.35 = (f32[64,256]{1,0:T(8,128)S(1)}, f32[64,256]{1,0:T(8,128)S(1)}, u32[]{:S(2)}, u32[]{:S(2)}) collective-permute-start(f32[64,256]{1,0:T(8,128)S(1)} %collective-permute-done.33), channel_id=1, source_target_pairs={{0,4},{1,5},{2,6},{3,7},{4,0},{5,1},{6,2},{7,3},{8,12},{9,13},{10,... | collective-permute-start | bytes 196616 | tf_op jit(solution)/shard_map/ppermute | solution.py:20
  139.7 2.3 %collective-permute-start.36 = (f32[64,256]{1,0:T(8,128)S(1)}, f32[64,256]{1,0:T(8,128)S(1)}, u32[]{:S(2)}, u32[]{:S(2)}) collective-permute-start(f32[64,256]{1,0:T(8,128)S(1)} %collective-permute-done.33), channel_id=1, source_target_pairs={{0,6},{1,7},{2,4},{3,5},{4,2},{5,3},{6,0},{7,1},{8,14},{9,15},{10,... | collective-permute-start | bytes 196616 | tf_op jit(solution)/shard_map/ppermute | solution.py:20
  143.0 2.8 %collective-permute-done.36 = f32[64,256]{1,0:T(8,128)S(1)} collective-permute-done((f32[64,256]{1,0:T(8,128)S(1)}, f32[64,256]{1,0:T(8,128)S(1)}, u32[]{:S(2)}, u32[]{:S(2)}) %collective-permute-start.36) | collective-permute-done | bytes 65568 | tf_op jit(solution)/shard_map/ppermute | solution.py:20
  (103 shorter events, 25.4 us)
Async XLA Ops:
  3.4 13.0 %copy-start = (f32[6,256,256]{2,1,0:T(8,128)S(1)}, f32[6,256,256]{2,1,0:T(8,128)}, u32[]{:S(2)}) copy-start(f32[6,256,256]{2,1,0:T(8,128)} %param.11) | copy-start | bytes 4718596
  3.7 10.2 %collective-permute-start.6 = (f32[256,256]{1,0:T(8,128)S(1)}, f32[256,256]{1,0:T(8,128)S(1)}, u32[]{:S(2)}, u32[]{:S(2)}) collective-permute-start(f32[256,256]{1,0:T(8,128)S(1)} %convolution_select_fusion), channel_id=1, source_target_pairs={{0,8},{8,0},{16,24},{24,16},{1,9},{9,1},{17,25},{25,17},{2,10},{10... | collective-permute-start | bytes 786440 | tf_op jit(solution)/shard_map/ppermute | solution.py:20
  6.9 9.9 %collective-permute-start.5 = (f32[6]{0:T(128)S(1)}, f32[6]{0:T(128)S(1)}, u32[]{:S(2)}, u32[]{:S(2)}) collective-permute-start(f32[6]{0:T(128)S(1)} %get-tuple-element.6), channel_id=1, source_target_pairs={{0,1},{1,0},{2,3},{3,2},{4,5},{5,4},{6,7},{7,6},{8,9},{9,8},{10,11... | collective-permute-start | bytes 80 | tf_op jit(solution)/shard_map/ppermute | solution.py:20
  12.0 12.3 %collective-permute-start = (f32[384,256]{1,0:T(8,128)}, f32[384,256]{1,0:T(8,128)}, u32[]{:S(2)}, u32[]{:S(2)}) collective-permute-start(f32[384,256]{1,0:T(8,128)} %get-tuple-element.17), channel_id=1, source_target_pairs={{0,1},{1,0},{2,3},{3,2},{4,5},{5,4},{6,7},{7,6},{8,9},{9,8},{10,11... | collective-permute-start | bytes 1179656 | tf_op jit(solution)/shard_map/ppermute | solution.py:20
  12.0 19.9 %collective-permute-start.1 = (f32[384,256]{1,0:T(8,128)}, f32[384,256]{1,0:T(8,128)}, u32[]{:S(2)}, u32[]{:S(2)}) collective-permute-start(f32[384,256]{1,0:T(8,128)} %get-tuple-element.18), channel_id=1, source_target_pairs={{0,1},{1,0},{2,3},{3,2},{4,5},{5,4},{6,7},{7,6},{8,9},{9,8},{10,11... | collective-permute-start | bytes 1179656 | tf_op jit(solution)/shard_map/ppermute | solution.py:20
  15.0 18.4 %collective-permute-start.7 = (f32[256,256]{1,0:T(8,128)}, f32[256,256]{1,0:T(8,128)}, u32[]{:S(2)}, u32[]{:S(2)}) collective-permute-start(f32[256,256]{1,0:T(8,128)} %fusion.37), channel_id=1, source_target_pairs={{0,16},{8,24},{16,0},{24,8},{1,17},{9,25},{17,1},{25,9},{2,18},{10... | collective-permute-start | bytes 786440 | tf_op jit(solution)/shard_map/ppermute | solution.py:20
  24.3 17.2 %collective-permute-start.2 = (f32[384,256]{1,0:T(8,128)}, f32[384,256]{1,0:T(8,128)S(1)}, u32[]{:S(2)}, u32[]{:S(2)}) collective-permute-start(f32[384,256]{1,0:T(8,128)} %collective-permute-done), channel_id=1, source_target_pairs={{0,16},{8,24},{16,0},{24,8},{1,17},{9,25},{17,1},{25,9},{2,18},{10... | collective-permute-start | bytes 1179656 | tf_op jit(solution)/shard_map/ppermute | solution.py:20
  31.8 10.5 %collective-permute-start.3 = (f32[384,256]{1,0:T(8,128)}, f32[384,256]{1,0:T(8,128)S(1)}, u32[]{:S(2)}, u32[]{:S(2)}) collective-permute-start(f32[384,256]{1,0:T(8,128)} %collective-permute-done.1), channel_id=1, source_target_pairs={{0,16},{8,24},{16,0},{24,8},{1,17},{9,25},{17,1},{25,9},{2,18},{10... | collective-permute-start | bytes 1179656 | tf_op jit(solution)/shard_map/ppermute | solution.py:20
  36.0 2.0 %copy-start.1 = (f32[6,256,256]{2,1,0:T(8,128)S(1)}, f32[6,256,256]{2,1,0:T(8,128)}, u32[]{:S(2)}) copy-start(f32[6,256,256]{2,1,0:T(8,128)} %param.12) | copy-start | bytes 4718596
  40.8 7.3 %collective-permute-start.8 = (f32[256,256]{1,0:T(8,128)S(1)}, f32[256,256]{1,0:T(8,128)S(1)}, u32[]{:S(2)}, u32[]{:S(2)}) collective-permute-start(f32[256,256]{1,0:T(8,128)S(1)} %dynamic-slice_bitcast_fusion), channel_id=1, source_target_pairs={{0,1},{1,0},{2,3},{3,2},{4,5},{5,4},{6,7},{7,6},{8,9},{9,8},{10,11... | collective-permute-start | bytes 786440 | tf_op jit(solution)/shard_map/ppermute | solution.py:20
  43.5 23.1 %collective-permute-start.4 = (f32[6,256,256]{2,1,0:T(8,128)S(1)}, f32[6,256,256]{2,1,0:T(8,128)S(1)}, u32[]{:S(2)}, u32[]{:S(2)}) collective-permute-start(f32[6,256,256]{2,1,0:T(8,128)S(1)} %bitcast.234), channel_id=1, source_target_pairs={{0,8},{8,0},{16,24},{24,16},{1,9},{9,1},{17,25},{25,17},{2,10},{10... | collective-permute-start | bytes 4718600 | tf_op jit(solution)/shard_map/ppermute | solution.py:20
  48.2 6.9 %collective-permute-start.10 = (f32[64,256]{1,0:T(8,128)S(1)}, f32[64,256]{1,0:T(8,128)S(1)}, u32[]{:S(2)}, u32[]{:S(2)}) collective-permute-start(f32[64,256]{1,0:T(8,128)S(1)} %get-tuple-element.34), channel_id=1, source_target_pairs={{0,4},{1,5},{2,6},{3,7},{4,0},{5,1},{6,2},{7,3},{8,12},{9,13},{10,... | collective-permute-start | bytes 196616 | tf_op jit(solution)/shard_map/ppermute | solution.py:20
  50.8 6.2 %collective-permute-start.11 = (f32[64,256]{1,0:T(8,128)S(1)}, f32[64,256]{1,0:T(8,128)S(1)}, u32[]{:S(2)}, u32[]{:S(2)}) collective-permute-start(f32[64,256]{1,0:T(8,128)S(1)} %get-tuple-element.33), channel_id=1, source_target_pairs={{0,6},{1,7},{2,4},{3,5},{4,2},{5,3},{6,0},{7,1},{8,14},{9,15},{10,... | collective-permute-start | bytes 196616 | tf_op jit(solution)/shard_map/ppermute | solution.py:20
  52.2 5.1 %collective-permute-start.9 = (f32[64,256]{1,0:T(8,128)S(1)}, f32[64,256]{1,0:T(8,128)S(1)}, u32[]{:S(2)}, u32[]{:S(2)}) collective-permute-start(f32[64,256]{1,0:T(8,128)S(1)} %get-tuple-element.32), channel_id=1, source_target_pairs={{0,2},{1,3},{2,0},{3,1},{4,6},{5,7},{6,4},{7,5},{8,10},{9,11},{10,... | collective-permute-start | bytes 196616 | tf_op jit(solution)/shard_map/ppermute | solution.py:20
  57.3 5.0 %collective-permute-start.12 = (f32[64,256]{1,0:T(8,128)S(1)}, f32[64,256]{1,0:T(8,128)S(1)}, u32[]{:S(2)}, u32[]{:S(2)}) collective-permute-start(f32[64,256]{1,0:T(8,128)S(1)} %get-tuple-element.14), channel_id=1, source_target_pairs={{0,2},{1,3},{2,0},{3,1},{4,6},{5,7},{6,4},{7,5},{8,10},{9,11},{10,... | collective-permute-start | bytes 196616 | tf_op jit(solution)/shard_map/ppermute | solution.py:20
  57.8 5.2 %collective-permute-start.13 = (f32[64,256]{1,0:T(8,128)S(1)}, f32[64,256]{1,0:T(8,128)S(1)}, u32[]{:S(2)}, u32[]{:S(2)}) collective-permute-start(f32[64,256]{1,0:T(8,128)S(1)} %get-tuple-element.14), channel_id=1, source_target_pairs={{0,4},{1,5},{2,6},{3,7},{4,0},{5,1},{6,2},{7,3},{8,12},{9,13},{10,... | collective-permute-start | bytes 196616 | tf_op jit(solution)/shard_map/ppermute | solution.py:20
  60.5 6.1 %collective-permute-start.14 = (f32[64,256]{1,0:T(8,128)S(1)}, f32[64,256]{1,0:T(8,128)S(1)}, u32[]{:S(2)}, u32[]{:S(2)}) collective-permute-start(f32[64,256]{1,0:T(8,128)S(1)} %get-tuple-element.14), channel_id=1, source_target_pairs={{0,6},{1,7},{2,4},{3,5},{4,2},{5,3},{6,0},{7,1},{8,14},{9,15},{10,... | collective-permute-start | bytes 196616 | tf_op jit(solution)/shard_map/ppermute | solution.py:20
  74.7 4.5 %collective-permute-start.15 = (f32[64,256]{1,0:T(8,128)S(1)}, f32[64,256]{1,0:T(8,128)S(1)}, u32[]{:S(2)}, u32[]{:S(2)}) collective-permute-start(f32[64,256]{1,0:T(8,128)S(1)} %get-tuple-element.29), channel_id=1, source_target_pairs={{0,2},{1,3},{2,0},{3,1},{4,6},{5,7},{6,4},{7,5},{8,10},{9,11},{10,... | collective-permute-start | bytes 196616 | tf_op jit(solution)/shard_map/ppermute | solution.py:20
  74.8 5.2 %collective-permute-start.16 = (f32[64,256]{1,0:T(8,128)S(1)}, f32[64,256]{1,0:T(8,128)S(1)}, u32[]{:S(2)}, u32[]{:S(2)}) collective-permute-start(f32[64,256]{1,0:T(8,128)S(1)} %get-tuple-element.31), channel_id=1, source_target_pairs={{0,4},{1,5},{2,6},{3,7},{4,0},{5,1},{6,2},{7,3},{8,12},{9,13},{10,... | collective-permute-start | bytes 196616 | tf_op jit(solution)/shard_map/ppermute | solution.py:20
  77.0 6.6 %collective-permute-start.17 = (f32[64,256]{1,0:T(8,128)S(1)}, f32[64,256]{1,0:T(8,128)S(1)}, u32[]{:S(2)}, u32[]{:S(2)}) collective-permute-start(f32[64,256]{1,0:T(8,128)S(1)} %get-tuple-element.30), channel_id=1, source_target_pairs={{0,6},{1,7},{2,4},{3,5},{4,2},{5,3},{6,0},{7,1},{8,14},{9,15},{10,... | collective-permute-start | bytes 196616 | tf_op jit(solution)/shard_map/ppermute | solution.py:20
  83.7 4.5 %collective-permute-start.18 = (f32[64,256]{1,0:T(8,128)S(1)}, f32[64,256]{1,0:T(8,128)S(1)}, u32[]{:S(2)}, u32[]{:S(2)}) collective-permute-start(f32[64,256]{1,0:T(8,128)S(1)} %get-tuple-element.12), channel_id=1, source_target_pairs={{0,2},{1,3},{2,0},{3,1},{4,6},{5,7},{6,4},{7,5},{8,10},{9,11},{10,... | collective-permute-start | bytes 196616 | tf_op jit(solution)/shard_map/ppermute | solution.py:20
  83.8 5.2 %collective-permute-start.19 = (f32[64,256]{1,0:T(8,128)S(1)}, f32[64,256]{1,0:T(8,128)S(1)}, u32[]{:S(2)}, u32[]{:S(2)}) collective-permute-start(f32[64,256]{1,0:T(8,128)S(1)} %get-tuple-element.12), channel_id=1, source_target_pairs={{0,4},{1,5},{2,6},{3,7},{4,0},{5,1},{6,2},{7,3},{8,12},{9,13},{10,... | collective-permute-start | bytes 196616 | tf_op jit(solution)/shard_map/ppermute | solution.py:20
  85.9 6.6 %collective-permute-start.20 = (f32[64,256]{1,0:T(8,128)S(1)}, f32[64,256]{1,0:T(8,128)S(1)}, u32[]{:S(2)}, u32[]{:S(2)}) collective-permute-start(f32[64,256]{1,0:T(8,128)S(1)} %get-tuple-element.12), channel_id=1, source_target_pairs={{0,6},{1,7},{2,4},{3,5},{4,2},{5,3},{6,0},{7,1},{8,14},{9,15},{10,... | collective-permute-start | bytes 196616 | tf_op jit(solution)/shard_map/ppermute | solution.py:20
  95.8 7.2 %collective-permute-start.21 = (f32[64,256]{1,0:T(8,128)S(1)}, f32[64,256]{1,0:T(8,128)S(1)}, u32[]{:S(2)}, u32[]{:S(2)}) collective-permute-start(f32[64,256]{1,0:T(8,128)S(1)} %get-tuple-element.26), channel_id=1, source_target_pairs={{0,2},{1,3},{2,0},{3,1},{4,6},{5,7},{6,4},{7,5},{8,10},{9,11},{10,... | collective-permute-start | bytes 196616 | tf_op jit(solution)/shard_map/ppermute | solution.py:20
  95.8 7.1 %collective-permute-start.22 = (f32[64,256]{1,0:T(8,128)S(1)}, f32[64,256]{1,0:T(8,128)S(1)}, u32[]{:S(2)}, u32[]{:S(2)}) collective-permute-start(f32[64,256]{1,0:T(8,128)S(1)} %get-tuple-element.28), channel_id=1, source_target_pairs={{0,4},{1,5},{2,6},{3,7},{4,0},{5,1},{6,2},{7,3},{8,12},{9,13},{10,... | collective-permute-start | bytes 196616 | tf_op jit(solution)/shard_map/ppermute | solution.py:20
  98.8 6.6 %collective-permute-start.23 = (f32[64,256]{1,0:T(8,128)S(1)}, f32[64,256]{1,0:T(8,128)S(1)}, u32[]{:S(2)}, u32[]{:S(2)}) collective-permute-start(f32[64,256]{1,0:T(8,128)S(1)} %get-tuple-element.27), channel_id=1, source_target_pairs={{0,6},{1,7},{2,4},{3,5},{4,2},{5,3},{6,0},{7,1},{8,14},{9,15},{10,... | collective-permute-start | bytes 196616 | tf_op jit(solution)/shard_map/ppermute | solution.py:20
  105.5 7.4 %collective-permute-start.24 = (f32[64,256]{1,0:T(8,128)S(1)}, f32[64,256]{1,0:T(8,128)S(1)}, u32[]{:S(2)}, u32[]{:S(2)}) collective-permute-start(f32[64,256]{1,0:T(8,128)S(1)} %get-tuple-element.10), channel_id=1, source_target_pairs={{0,2},{1,3},{2,0},{3,1},{4,6},{5,7},{6,4},{7,5},{8,10},{9,11},{10,... | collective-permute-start | bytes 196616 | tf_op jit(solution)/shard_map/ppermute | solution.py:20
  109.6 8.3 %collective-permute-start.25 = (f32[64,256]{1,0:T(8,128)S(1)}, f32[64,256]{1,0:T(8,128)S(1)}, u32[]{:S(2)}, u32[]{:S(2)}) collective-permute-start(f32[64,256]{1,0:T(8,128)S(1)} %get-tuple-element.10), channel_id=1, source_target_pairs={{0,4},{1,5},{2,6},{3,7},{4,0},{5,1},{6,2},{7,3},{8,12},{9,13},{10,... | collective-permute-start | bytes 196616 | tf_op jit(solution)/shard_map/ppermute | solution.py:20
  110.4 7.5 %collective-permute-start.26 = (f32[64,256]{1,0:T(8,128)S(1)}, f32[64,256]{1,0:T(8,128)S(1)}, u32[]{:S(2)}, u32[]{:S(2)}) collective-permute-start(f32[64,256]{1,0:T(8,128)S(1)} %get-tuple-element.10), channel_id=1, source_target_pairs={{0,6},{1,7},{2,4},{3,5},{4,2},{5,3},{6,0},{7,1},{8,14},{9,15},{10,... | collective-permute-start | bytes 196616 | tf_op jit(solution)/shard_map/ppermute | solution.py:20
  120.8 6.6 %copy-start.2 = (f32[1,2,256,256]{3,2,1,0:T(8,128)S(1)}, f32[1,2,256,256]{3,2,1,0:T(8,128)}, u32[]{:S(2)}) copy-start(f32[1,2,256,256]{3,2,1,0:T(8,128)} %param.8) | copy-start | bytes 1572868
  122.5 5.4 %collective-permute-start.27 = (f32[64,256]{1,0:T(8,128)S(1)}, f32[64,256]{1,0:T(8,128)S(1)}, u32[]{:S(2)}, u32[]{:S(2)}) collective-permute-start(f32[64,256]{1,0:T(8,128)S(1)} %get-tuple-element.23), channel_id=1, source_target_pairs={{0,2},{1,3},{2,0},{3,1},{4,6},{5,7},{6,4},{7,5},{8,10},{9,11},{10,... | collective-permute-start | bytes 196616 | tf_op jit(solution)/shard_map/ppermute | solution.py:20
  124.5 7.0 %collective-permute-start.28 = (f32[64,256]{1,0:T(8,128)S(1)}, f32[64,256]{1,0:T(8,128)S(1)}, u32[]{:S(2)}, u32[]{:S(2)}) collective-permute-start(f32[64,256]{1,0:T(8,128)S(1)} %get-tuple-element.25), channel_id=1, source_target_pairs={{0,4},{1,5},{2,6},{3,7},{4,0},{5,1},{6,2},{7,3},{8,12},{9,13},{10,... | collective-permute-start | bytes 196616 | tf_op jit(solution)/shard_map/ppermute | solution.py:20
  124.6 7.0 %collective-permute-start.29 = (f32[64,256]{1,0:T(8,128)S(1)}, f32[64,256]{1,0:T(8,128)S(1)}, u32[]{:S(2)}, u32[]{:S(2)}) collective-permute-start(f32[64,256]{1,0:T(8,128)S(1)} %get-tuple-element.24), channel_id=1, source_target_pairs={{0,6},{1,7},{2,4},{3,5},{4,2},{5,3},{6,0},{7,1},{8,14},{9,15},{10,... | collective-permute-start | bytes 196616 | tf_op jit(solution)/shard_map/ppermute | solution.py:20
  131.6 5.9 %collective-permute-start.33 = (f32[64,256]{1,0:T(8,128)S(1)}, f32[64,256]{1,0:T(8,128)S(1)}, u32[]{:S(2)}, u32[]{:S(2)}) collective-permute-start(f32[64,256]{1,0:T(8,128)S(1)} %get-tuple-element.8), channel_id=1, source_target_pairs={{0,1},{1,0},{2,3},{3,2},{4,5},{5,4},{6,7},{7,6},{8,9},{9,8},{10,11... | collective-permute-start | bytes 196616 | tf_op jit(solution)/shard_map/ppermute | solution.py:20
  133.1 6.6 %collective-permute-start.30 = (f32[64,256]{1,0:T(8,128)S(1)}, f32[64,256]{1,0:T(8,128)S(1)}, u32[]{:S(2)}, u32[]{:S(2)}) collective-permute-start(f32[64,256]{1,0:T(8,128)S(1)} %get-tuple-element.8), channel_id=1, source_target_pairs={{0,2},{1,3},{2,0},{3,1},{4,6},{5,7},{6,4},{7,5},{8,10},{9,11},{10,... | collective-permute-start | bytes 196616 | tf_op jit(solution)/shard_map/ppermute | solution.py:20
  134.4 7.6 %collective-permute-start.31 = (f32[64,256]{1,0:T(8,128)S(1)}, f32[64,256]{1,0:T(8,128)S(1)}, u32[]{:S(2)}, u32[]{:S(2)}) collective-permute-start(f32[64,256]{1,0:T(8,128)S(1)} %get-tuple-element.8), channel_id=1, source_target_pairs={{0,4},{1,5},{2,6},{3,7},{4,0},{5,1},{6,2},{7,3},{8,12},{9,13},{10,... | collective-permute-start | bytes 196616 | tf_op jit(solution)/shard_map/ppermute | solution.py:20
  135.2 6.8 %collective-permute-start.32 = (f32[64,256]{1,0:T(8,128)S(1)}, f32[64,256]{1,0:T(8,128)S(1)}, u32[]{:S(2)}, u32[]{:S(2)}) collective-permute-start(f32[64,256]{1,0:T(8,128)S(1)} %get-tuple-element.8), channel_id=1, source_target_pairs={{0,6},{1,7},{2,4},{3,5},{4,2},{5,3},{6,0},{7,1},{8,14},{9,15},{10,... | collective-permute-start | bytes 196616 | tf_op jit(solution)/shard_map/ppermute | solution.py:20
  137.5 4.6 %collective-permute-start.34 = (f32[64,256]{1,0:T(8,128)S(1)}, f32[64,256]{1,0:T(8,128)S(1)}, u32[]{:S(2)}, u32[]{:S(2)}) collective-permute-start(f32[64,256]{1,0:T(8,128)S(1)} %collective-permute-done.33), channel_id=1, source_target_pairs={{0,2},{1,3},{2,0},{3,1},{4,6},{5,7},{6,4},{7,5},{8,10},{9,11},{10,... | collective-permute-start | bytes 196616 | tf_op jit(solution)/shard_map/ppermute | solution.py:20
  137.8 5.2 %collective-permute-start.35 = (f32[64,256]{1,0:T(8,128)S(1)}, f32[64,256]{1,0:T(8,128)S(1)}, u32[]{:S(2)}, u32[]{:S(2)}) collective-permute-start(f32[64,256]{1,0:T(8,128)S(1)} %collective-permute-done.33), channel_id=1, source_target_pairs={{0,4},{1,5},{2,6},{3,7},{4,0},{5,1},{6,2},{7,3},{8,12},{9,13},{10,... | collective-permute-start | bytes 196616 | tf_op jit(solution)/shard_map/ppermute | solution.py:20
  139.7 6.1 %collective-permute-start.36 = (f32[64,256]{1,0:T(8,128)S(1)}, f32[64,256]{1,0:T(8,128)S(1)}, u32[]{:S(2)}, u32[]{:S(2)}) collective-permute-start(f32[64,256]{1,0:T(8,128)S(1)} %collective-permute-done.33), channel_id=1, source_target_pairs={{0,6},{1,7},{2,4},{3,5},{4,2},{5,3},{6,0},{7,1},{8,14},{9,15},{10,... | collective-permute-start | bytes 196616 | tf_op jit(solution)/shard_map/ppermute | solution.py:20
where the time goes:
time: 147 us
  starting transfers between devices  51.8 us (35%)
  waiting for transfers between devices  51.4 us (35%)
  matrix products  33.7 us (23%)
  other arithmetic  7.03 us (5%)
  local copies, waits for them, and re-layouts  1.47 us (1%)
    ppermute x37, starting transfers between devices, swap(): return lax.ppermute(value, axis, pairs)  51.8 us
    ppermute x37, waiting for transfers between devices, swap(): return lax.ppermute(value, axis, pairs)  51.4 us
    dot_general x11, matrix products, product(): jnp.dot(left, right, precision=lax.Precision.HIGH, preferred_element_type...  13.3 us
    dot_general x3, matrix products, apply_terms(): jnp.einsum('tik,tkl->il', lefted, rights, precision=lax.Precision.HIGH, p...  5.14 us
  transfers between devices with their start and end apart: 37, of which 20 were waited for; matrix products, arithmetic and copies ran while one was open for 15% of the time, Pallas kernels for 0%

commit v1 on v0

v1 whole, which is shorter than its diff:
```python
import jax
import jax.numpy as jnp
from jax import lax
from jax.sharding import PartitionSpec as P

ORDER = 4
TAYLOR_STEP = 0.3
PAIR = 2


def product(left, right):
    return jnp.dot(left, right, precision=lax.Precision.HIGH, preferred_element_type=jnp.float32)


def contract(spec, left, right):
    return jnp.einsum(
        spec, left, right, precision=lax.Precision.HIGH, preferred_element_type=jnp.float32
    )


def swap(value, axis, mask):
    pairs = [(i, i ^ mask) for i in range(lax.axis_size(axis))]
    return lax.ppermute(value, axis, pairs)


def sum_masks():
    size = lax.axis_size("term")
    masks = [1]
    if size >= 8:
        masks.append(6)
    bit = 8
    while bit < size:
        masks.append(bit)
        bit *= 2
    return masks


def section_product(slots, count):
    factors = [slots[i] for i in range(slots.shape[0])]
    starts = list(range(len(factors)))
    while len(factors) > 1:
        merged, merged_starts = [], []
        for i in range(0, len(factors), 2):
            if i + 1 == len(factors):
                merged.append(factors[i])
            else:
                both = product(factors[i], factors[i + 1])
                merged.append(jnp.where(starts[i + 1] < count, both, factors[i]))
            merged_starts.append(starts[i])
        factors, starts = merged, merged_starts
    return factors[0]


def scan_maps(section_map):
    position = lax.axis_index("sec")
    sections = lax.axis_size("sec")
    segment = section_map
    identity = jnp.eye(section_map.shape[0], dtype=jnp.float32)
    prefix = suffix = identity
    bit = 1
    while bit < sections:
        other = swap(segment, "sec", bit)
        upper = (position & bit) != 0
        if bit == 1:
            prefix = jnp.where(upper, other, identity)
            suffix = jnp.where(upper, identity, other)
        else:
            grown = product(jnp.where(upper, other, suffix), jnp.where(upper, prefix, other))
            prefix = jnp.where(upper, grown, prefix)
            suffix = jnp.where(upper, suffix, grown)
        if 2 * bit < sections:
            segment = product(
                jnp.where(upper, other, segment), jnp.where(upper, segment, other)
            )
        bit *= 2
    return prefix, suffix


def sum_groups(partial):
    masks = sum_masks()
    half = partial.shape[0] // 2
    upper, lower = partial[:half], partial[half:]
    for i in range(len(masks)):
        upper, lower = (
            upper + swap(upper, "term", masks[i]), lower + swap(lower, "term", masks[-1 - i])
        )
    return upper, lower


def apply_terms(tensor, lefts, rights):
    return contract("tik,tkl->il", contract("tij,jk->tik", lefts, tensor), rights)


def on_device(
    center, site_maps, section_sites, left_edge, right_edge, coefficients, term_ids, sector_mask
):
    width = center.shape[2]
    slots = left_edge.shape[0]
    half = slots // 2
    piece = half * width // 2
    place = lax.axis_index("term")
    mine = ((place >> 1) ^ (place >> 2)) & 1
    spot = lax.axis_index("sec")
    core, side = spot & 1, (spot >> 1) & 1

    chosen = term_ids[:, None] == jnp.arange(coefficients.shape[0], dtype=jnp.int32)[None, :]
    slot_weight = jnp.sum(jnp.where(chosen, coefficients[None, :], 0.0), axis=1)
    slot_mask = jnp.sum(
        jnp.where(chosen[:, :, None], sector_mask.astype(jnp.float32)[None], 0.0), axis=1
    )
    weight = slot_weight[:, None] * slot_mask
    keep_weight = jnp.where(mine == 0, weight[:, 0], weight[:, 1])
    give_weight = jnp.where(mine == 0, weight[:, 1], weight[:, 0])

    flat_left = left_edge.reshape(slots * width, width)
    flat_right = right_edge.reshape(slots * width, width)
    pieces = []
    for i in range(2):
        start = side * (half * width) + i * piece
        cut = jnp.where(
            core == 0,
            lax.dynamic_slice_in_dim(flat_left, start, piece, 0),
            lax.dynamic_slice_in_dim(flat_right, start, piece, 0),
        )
        pieces.append(swap(cut, "term", PAIR))
    shared = [swap(pieces[i], "sec", 2) for i in range(2)]
    halves = jnp.concatenate(pieces + shared, axis=0).reshape(slots, width, width)
    traded = swap(halves, "sec", 1)
    others = swap(give_weight, "term", PAIR)
    others = jnp.where(side == 0, others, jnp.roll(others, half))
    other_left = jnp.where(core == 0, halves, traded) * others[:, None, None]
    other_right = jnp.where(core == 0, traded, halves)

    section_map = section_product(site_maps, section_sites[0])
    prefix, suffix = scan_maps(section_map)

    base = center[0]
    start_keep = lax.dynamic_index_in_dim(base, mine, 0, keepdims=False)
    start_give = lax.dynamic_index_in_dim(base, 1 - mine, 0, keepdims=False)

    def first(start, weights):
        turned = product(product(prefix, start), suffix)
        lefted = contract("tij,jk->tik", left_edge, turned) * weights[:, None, None]
        return contract("tik,tkl->il", lefted, right_edge)

    given = first(start_give, give_weight)
    kept = first(start_keep, keep_weight)
    partial = kept + swap(given, "term", PAIR)
    current = jnp.concatenate(sum_groups(partial), axis=0) * (-TAYLOR_STEP)
    total = current

    gram_left = contract("ij,kj->ik", prefix, prefix)
    gram_right = contract("ji,jk->ik", suffix, suffix)
    own_left = left_edge * keep_weight[:, None, None]

    turned = product(product(gram_left, current), gram_right)
    partial = apply_terms(turned, own_left, right_edge)
    partial = partial + apply_terms(turned, other_left, other_right)
    current = jnp.concatenate(sum_groups(partial), axis=0) * (-TAYLOR_STEP / 2)
    total = total + current

    lefts = jnp.concatenate([own_left, other_left], axis=0)
    rights = jnp.concatenate([right_edge, other_right], axis=0)
    lefts = contract("tij,jk->tik", lefts, gram_left)
    rights = contract("ij,tjk->tik", gram_right, rights)
    lefts_out = contract("ji,tjk->tik", prefix, lefts)
    rights_out = contract("tij,kj->tik", rights, suffix)

    for order in range(3, ORDER):
        partial = apply_terms(current, lefts, rights)
        current = jnp.concatenate(sum_groups(partial), axis=0)
        current = current * (-TAYLOR_STEP / order)
        total = total + current

    partial = apply_terms(current, lefts_out, rights_out) * (-TAYLOR_STEP / ORDER)
    so_far = start_keep + contract("ij,kj->ik", contract("ji,jk->ik", prefix, total), suffix)
    ends = sum_groups(partial)
    ours, theirs = [], []
    for i, end in enumerate(ends):
        rows = end.shape[0]
        end = so_far[i * rows : (i + 1) * rows] + end
        ours.append(end)
        theirs.append(swap(end, "term", PAIR))
    ours, theirs = jnp.concatenate(ours, axis=0), jnp.concatenate(theirs, axis=0)
    evolved = jnp.stack(
        [jnp.where(mine == 0, ours, theirs), jnp.where(mine == 0, theirs, ours)]
    )
    return evolved[None]


def solution(mesh):
    in_specs = (
        P("sec", None, None, None),
        P("sec", None, None),
        P("sec"),
        P("term", None, None),
        P("term", None, None),
        P(),
        P("term"),
        P(),
    )
    out_specs = P("sec", None, None, None)
    return jax.shard_map(
        on_device, mesh=mesh, in_specs=in_specs, out_specs=out_specs, check_vma=False
    )
```

time: 147 us -> 127 us (0.86)
  starting transfers between devices: 51.8 us -> 39.3 us
  waiting for transfers between devices: 51.4 us -> 45.5 us
    ppermute x37 -> x27, starting transfers between devices: 51.8 us -> 39.3 us  [swap(): return lax.ppermute(value, axis, pairs)]
    dot_general x12 -> x20, matrix products: 20.5 us -> 27.1 us  [contract(): jnp.einsum(spec, left, right, precision=lax.Precision.HIGH, preferred_ele...]
    dot_general x11, matrix products: 13.3 us -> 7.25 us  [product(): jnp.dot(left, right, precision=lax.Precision.HIGH, preferred_element_type...]
    ppermute x37 -> x27, waiting for transfers between devices: 51.4 us -> 45.5 us  [swap(): return lax.ppermute(value, axis, pairs)]
  transfers between devices with their start and end apart: 37 -> 27, of which waited for: 20 -> 17; matrix products, arithmetic and copies ran while one was open for 15% -> 20% of each run, Pallas kernels for 0% -> 0%
where the time goes in v1:
time: 127 us; the launch traced here: 126 us
  waiting for transfers between devices  45.5 us (36%)
  starting transfers between devices  39.3 us (31%)
  matrix products  34.4 us (27%)
  other arithmetic  5.7 us (4%)
    ppermute x27, waiting for transfers between devices, swap(): return lax.ppermute(value, axis, pairs)  45.5 us
    ppermute x27, starting transfers between devices, swap(): return lax.ppermute(value, axis, pairs)  39.3 us
    dot_general x20, matrix products, contract(): jnp.einsum(spec, left, right, precision=lax.Precision.HIGH, preferred_ele...  27.1 us
    dot_general x11, matrix products, product(): jnp.dot(left, right, precision=lax.Precision.HIGH, preferred_element_type...  7.25 us
  transfers between devices with their start and end apart: 27, of which 17 were waited for; matrix products, arithmetic and copies ran while one was open for 20% of the time, Pallas kernels for 0%

profile of v1, /device:TPU:0, one launch (start us, length us, event | category | flops | bytes accessed | tf_op | source)
XLA Modules:
  0.0 126.3 jit_solution(4715060504771035547)
XLA Ops:
  0.8 1.4 %convolution_select_fusion.1 = f32[256,256]{1,0:T(8,128)S(1)} fusion(f32[4,256,256]{2,1,0:T(8,128)} %param.9, pred[]{:T(512)} %bitcast.5), kind=kOutput, calls=%fused_computation.23 | convolution fusion | flops 100728832 | bytes 1049088 | tf_op jit(solution)/shard_map/dot_general | solution.py:12
  2.2 1.4 %convolution_select_fusion.2 = f32[256,256]{1,0:T(8,128)S(1)} fusion(f32[4,256,256]{2,1,0:T(8,128)} %param.9, pred[]{:T(512)} %bitcast.2), kind=kOutput, calls=%fused_computation.24 | convolution fusion | flops 100728832 | bytes 1049088 | tf_op jit(solution)/shard_map/dot_general | solution.py:12
  3.6 1.0 convolution_select_fusion
  5.1 2.1 %dynamic-slice_select_fusion.1 = (f32[384,256]{1,0:T(8,128)}, f32[384,256]{1,0:T(8,128)}) fusion(f32[1536,256]{1,0:T(8,128)S(1)} %bitcast.132, s32[]{:T(128)S(6)} %select_n.187, f32[1536,256]{1,0:T(8,128)} %bitcast.133, pred[]{:T(512)S(6)} %eq.42, s32[]{:T(128)S(6)} %select_n.189), kind=kLoop, calls=%fused_computation.44 | loop fusion | flops 196608 | bytes 2359305 | tf_op jit(solution)/shard_map/jit(_where)/select_n | solution.py:120
  7.2 2.6 %collective-permute-start.8 = (f32[384,256]{1,0:T(8,128)}, f32[384,256]{1,0:T(8,128)}, u32[]{:S(2)}, u32[]{:S(2)}) collective-permute-start(f32[384,256]{1,0:T(8,128)} %get-tuple-element.10), channel_id=1, source_target_pairs={{0,2},{1,3},{2,0},{3,1},{4,6},{5,7},{6,4},{7,5},{8,10},{9,11},{10,... | collective-permute-start | bytes 1179656 | tf_op jit(solution)/shard_map/ppermute | solution.py:23
  10.4 2.1 %collective-permute-start.12 = (f32[6]{0:T(128)S(1)}, f32[6]{0:T(128)S(1)}, u32[]{:S(2)}, u32[]{:S(2)}) collective-permute-start(f32[6]{0:T(128)S(1)} %get-tuple-element.6), channel_id=1, source_target_pairs={{0,2},{1,3},{2,0},{3,1},{4,6},{5,7},{6,4},{7,5},{8,10},{9,11},{10,... | collective-permute-start | bytes 80 | tf_op jit(solution)/shard_map/ppermute | solution.py:23
  12.7 1.3 %fusion.59 = f32[256,256]{1,0:T(8,128)S(1)} fusion(f32[256,256]{1,0:T(8,128)} %convolution_select_fusion, f32[256,256]{1,0:T(8,128)S(1)} %collective-permute-done, pred[]{:T(512)S(6)} %ne.7), kind=kOutput, calls=%fused_computation.76 | convolution fusion | flops 100794368 | bytes 786433 | tf_op jit(solution)/shard_map/dot_general | solution.py:12
  14.0 1.6 %collective-permute-start.1 = (f32[256,256]{1,0:T(8,128)S(1)}, f32[256,256]{1,0:T(8,128)S(1)}, u32[]{:S(2)}, u32[]{:S(2)}) collective-permute-start(f32[256,256]{1,0:T(8,128)S(1)} %fusion.59), channel_id=1, source_target_pairs={{0,16},{8,24},{16,0},{24,8},{1,17},{9,25},{17,1},{25,9},{2,18},{10... | collective-permute-start | bytes 786440 | tf_op jit(solution)/shard_map/ppermute | solution.py:23
  15.6 12.7 %collective-permute-done.12 = f32[6]{0:T(128)S(1)} collective-permute-done((f32[6]{0:T(128)S(1)}, f32[6]{0:T(128)S(1)}, u32[]{:S(2)}, u32[]{:S(2)}) %collective-permute-start.12) | collective-permute-done | bytes 56 | tf_op jit(solution)/shard_map/ppermute | solution.py:23
  28.4 1.7 %collective-permute-start.10 = (f32[384,256]{1,0:T(8,128)}, f32[384,256]{1,0:T(8,128)S(1)}, u32[]{:S(2)}, u32[]{:S(2)}) collective-permute-start(f32[384,256]{1,0:T(8,128)} %collective-permute-done.8), channel_id=1, source_target_pairs={{0,16},{8,24},{16,0},{24,8},{1,17},{9,25},{17,1},{25,9},{2,18},{10... | collective-permute-start | bytes 1179656 | tf_op jit(solution)/shard_map/ppermute | solution.py:23
  32.3 1.5 %fusion.23 = f32[256,256]{1,0:T(8,128)S(1)} fusion(f32[6,256,256]{2,1,0:T(8,128)S(1)} %copy-done, f32[256,6,256]{2,0,1:T(8,128)S(1)} %fusion.101, f32[6]{0:T(128)S(1)} %get-tuple-element.6), kind=kOutput, calls=%fused_computation.26 | convolution fusion | flops 604372992 | bytes 3407896 | tf_op jit(solution)/shard_map/tik,tkl->il/dot_general | solution.py:16
  33.8 1.8 %collective-permute-start.2 = (f32[256,256]{1,0:T(8,128)S(1)}, f32[256,256]{1,0:T(8,128)S(1)}, u32[]{:S(2)}, u32[]{:S(2)}) collective-permute-start(f32[256,256]{1,0:T(8,128)S(1)} %fusion.23), channel_id=1, source_target_pairs={{0,2},{1,3},{2,0},{3,1},{4,6},{5,7},{6,4},{7,5},{8,10},{9,11},{10,... | collective-permute-start | bytes 786440 | tf_op jit(solution)/shard_map/ppermute | solution.py:23
  37.2 4.3 %collective-permute-done.2 = f32[256,256]{1,0:T(8,128)S(1)} collective-permute-done((f32[256,256]{1,0:T(8,128)S(1)}, f32[256,256]{1,0:T(8,128)S(1)}, u32[]{:S(2)}, u32[]{:S(2)}) %collective-permute-start.2) | collective-permute-done | bytes 262176 | tf_op jit(solution)/shard_map/ppermute | solution.py:23
  41.5 1.5 %fusion.30 = f32[256,256]{1,0:T(8,128)S(1)} fusion(f32[256,256]{1,0:T(8,128)S(1)} %collective-permute-done.2, f32[6,256,256]{2,1,0:T(8,128)S(1)} %copy-done, f32[256,6,256]{2,0,1:T(8,128)S(1)} %fusion.100, f32[6]{0:T(128)S(1)} %get-tuple-element.5), kind=kOutput, calls=%fused_computation.36 | convolution fusion | flops 604438528 | bytes 3670040 | tf_op jit(solution)/shard_map/tik,tkl->il/dot_general | solution.py:16
  43.0 1.4 %collective-permute-start.3 = (f32[128,256]{1,0:T(8,128)S(1)}, f32[128,256]{1,0:T(8,128)S(1)}, u32[]{:S(2)}, u32[]{:S(2)}) collective-permute-start(f32[128,256]{1,0:T(8,128)S(1)} %get-tuple-element.31), channel_id=1, source_target_pairs={{0,1},{1,0},{2,3},{3,2},{4,5},{5,4},{6,7},{7,6},{8,9},{9,8},{10,11... | collective-permute-start | bytes 393224 | tf_op jit(solution)/shard_map/ppermute | solution.py:23
  44.5 3.6 %collective-permute-start.5 = (f32[128,256]{1,0:T(8,128)S(1)}, f32[128,256]{1,0:T(8,128)S(1)}, u32[]{:S(2)}, u32[]{:S(2)}) collective-permute-start(f32[128,256]{1,0:T(8,128)S(1)} %get-tuple-element.32), channel_id=1, source_target_pairs={{0,6},{1,7},{2,4},{3,5},{4,2},{5,3},{6,0},{7,1},{8,14},{9,15},{10,... | collective-permute-start | bytes 393224 | tf_op jit(solution)/shard_map/ppermute | solution.py:23
  48.1 1.2 pad_maximum_fusion
  49.7 1.6 %collective-permute-done.5 = f32[128,256]{1,0:T(8,128)S(1)} collective-permute-done((f32[128,256]{1,0:T(8,128)S(1)}, f32[128,256]{1,0:T(8,128)S(1)}, u32[]{:S(2)}, u32[]{:S(2)}) %collective-permute-start.5) | collective-permute-done | bytes 131104 | tf_op jit(solution)/shard_map/ppermute | solution.py:23
  51.4 3.6 %collective-permute-start.4 = (f32[128,256]{1,0:T(8,128)S(1)}, f32[128,256]{1,0:T(8,128)S(1)}, u32[]{:S(2)}, u32[]{:S(2)}) collective-permute-start(f32[128,256]{1,0:T(8,128)S(1)} %get-tuple-element.29), channel_id=1, source_target_pairs={{0,6},{1,7},{2,4},{3,5},{4,2},{5,3},{6,0},{7,1},{8,14},{9,15},{10,... | collective-permute-start | bytes 393224 | tf_op jit(solution)/shard_map/ppermute | solution.py:23
  55.9 2.4 %collective-permute-done.4 = f32[128,256]{1,0:T(8,128)S(1)} collective-permute-done((f32[128,256]{1,0:T(8,128)S(1)}, f32[128,256]{1,0:T(8,128)S(1)}, u32[]{:S(2)}, u32[]{:S(2)}) %collective-permute-start.4) | collective-permute-done | bytes 131104 | tf_op jit(solution)/shard_map/ppermute | solution.py:23
  58.3 1.6 %collective-permute-done.6 = f32[128,256]{1,0:T(8,128)S(1)} collective-permute-done((f32[128,256]{1,0:T(8,128)S(1)}, f32[128,256]{1,0:T(8,128)S(1)}, u32[]{:S(2)}, u32[]{:S(2)}) %collective-permute-start.6) | collective-permute-done | bytes 131104 | tf_op jit(solution)/shard_map/ppermute | solution.py:23
  62.5 1.0 fusion.105
  63.5 0.9 fusion.33
  65.1 2.2 %collective-permute-start.15 = (f32[128,256]{1,0:T(8,128)S(1)}, f32[128,256]{1,0:T(8,128)S(1)}, u32[]{:S(2)}, u32[]{:S(2)}) collective-permute-start(f32[128,256]{1,0:T(8,128)S(1)} %get-tuple-element.28), channel_id=1, source_target_pairs={{0,6},{1,7},{2,4},{3,5},{4,2},{5,3},{6,0},{7,1},{8,14},{9,15},{10,... | collective-permute-start | bytes 393224 | tf_op jit(solution)/shard_map/ppermute | solution.py:23
  67.3 1.5 %fusion = f32[12,256,256]{2,1,0:T(8,128)S(1)} fusion(f32[6,256,256]{2,1,0:T(8,128)S(1)} %get-tuple-element.8, f32[6,256,256]{2,1,0:T(8,128)S(1)} %broadcast_multiply_fusion, f32[256,256]{1,0:T(8,128)S(1)} %fusion.102), kind=kOutput, calls=%fused_computation | convolution fusion | flops 1208745984 | bytes 6553600 | tf_op jit(solution)/shard_map/tij,jk->tik/dot_general | solution.py:16
  69.5 2.4 %collective-permute-done.15 = f32[128,256]{1,0:T(8,128)S(1)} collective-permute-done((f32[128,256]{1,0:T(8,128)S(1)}, f32[128,256]{1,0:T(8,128)S(1)}, u32[]{:S(2)}, u32[]{:S(2)}) %collective-permute-start.15) | collective-permute-done | bytes 131104 | tf_op jit(solution)/shard_map/ppermute | solution.py:23
  72.0 2.3 %collective-permute-start.14 = (f32[128,256]{1,0:T(8,128)S(1)}, f32[128,256]{1,0:T(8,128)S(1)}, u32[]{:S(2)}, u32[]{:S(2)}) collective-permute-start(f32[128,256]{1,0:T(8,128)S(1)} %get-tuple-element.25), channel_id=1, source_target_pairs={{0,6},{1,7},{2,4},{3,5},{4,2},{5,3},{6,0},{7,1},{8,14},{9,15},{10,... | collective-permute-start | bytes 393224 | tf_op jit(solution)/shard_map/ppermute | solution.py:23
  74.2 1.2 collective-permute-start.16
  75.5 2.7 %fusion.4 = f32[12,256,256]{2,1,0:T(8,128)S(1)} fusion(f32[6,256,256]{2,1,0:T(8,128)S(1)} %get-tuple-element.7, f32[6,256,256]{2,1,0:T(8,128)S(1)} %copy-done, f32[256,256]{1,0:T(8,128)S(1)} %fusion.103), kind=kOutput, calls=%fused_computation.4 | convolution fusion | flops 1208745984 | bytes 6553600 | tf_op jit(solution)/shard_map/ij,tjk->tik/dot_general | solution.py:16
  79.2 1.5 %fusion.41 = f32[12,256,256]{2,1,0:T(8,128)S(1)} fusion(f32[12,256,256]{2,1,0:T(8,128)S(1)} %fusion, f32[128,256]{1,0:T(8,128)S(1)} %add.104, f32[128,256]{1,0:T(8,128)S(1)} %add.102), kind=kOutput, calls=%fused_computation.57 | convolution fusion | flops 1208090624 | bytes 6553600 | tf_op jit(solution)/shard_map/tij,jk->tik/dot_general | solution.py:16
  80.7 1.7 %fusion.26 = f32[256,256]{1,0:T(8,128)S(1)} fusion(f32[12,256,256]{2,1,0:T(8,128)S(1)} %fusion.41, f32[12,256,256]{2,1,0:T(8,128)S(1)} %fusion.4), kind=kOutput, calls=%fused_computation.33 | convolution fusion | flops 1207959552 | bytes 6553600 | tf_op jit(solution)/shard_map/tik,tkl->il/dot_general | solution.py:16
  82.5 1.3 %collective-permute-start.17 = (f32[128,256]{1,0:T(8,128)S(1)}, f32[128,256]{1,0:T(8,128)S(1)}, u32[]{:S(2)}, u32[]{:S(2)}) collective-permute-start(f32[128,256]{1,0:T(8,128)S(1)} %get-tuple-element.23), channel_id=1, source_target_pairs={{0,1},{1,0},{2,3},{3,2},{4,5},{5,4},{6,7},{7,6},{8,9},{9,8},{10,11... | collective-permute-start | bytes 393224 | tf_op jit(solution)/shard_map/ppermute | solution.py:23
  83.8 1.9 %collective-permute-start.19 = (f32[128,256]{1,0:T(8,128)S(1)}, f32[128,256]{1,0:T(8,128)S(1)}, u32[]{:S(2)}, u32[]{:S(2)}) collective-permute-start(f32[128,256]{1,0:T(8,128)S(1)} %get-tuple-element.24), channel_id=1, source_target_pairs={{0,6},{1,7},{2,4},{3,5},{4,2},{5,3},{6,0},{7,1},{8,14},{9,15},{10,... | collective-permute-start | bytes 393224 | tf_op jit(solution)/shard_map/ppermute | solution.py:23
  85.7 2.7 %fusion.38 = f32[12,256,256]{2,1,0:T(8,128)S(1)} fusion(f32[12,256,256]{2,1,0:T(8,128)S(1)} %fusion, f32[256,256]{1,0:T(8,128)S(1)} %get-tuple-element.14), kind=kOutput, calls=%fused_computation.54 | convolution fusion | flops 1207959552 | bytes 6553600 | tf_op jit(solution)/shard_map/ji,tjk->tik/dot_general | solution.py:16
  88.4 3.5 %collective-permute-done.19 = f32[128,256]{1,0:T(8,128)S(1)} collective-permute-done((f32[128,256]{1,0:T(8,128)S(1)}, f32[128,256]{1,0:T(8,128)S(1)}, u32[]{:S(2)}, u32[]{:S(2)}) %collective-permute-start.19) | collective-permute-done | bytes 131104 | tf_op jit(solution)/shard_map/ppermute | solution.py:23
  92.0 2.1 %collective-permute-start.18 = (f32[128,256]{1,0:T(8,128)S(1)}, f32[128,256]{1,0:T(8,128)S(1)}, u32[]{:S(2)}, u32[]{:S(2)}) collective-permute-start(f32[128,256]{1,0:T(8,128)S(1)} %get-tuple-element.21), channel_id=1, source_target_pairs={{0,6},{1,7},{2,4},{3,5},{4,2},{5,3},{6,0},{7,1},{8,14},{9,15},{10,... | collective-permute-start | bytes 393224 | tf_op jit(solution)/shard_map/ppermute | solution.py:23
  94.1 2.9 %fusion.10 = f32[12,256,256]{2,1,0:T(8,128)S(1)} fusion(f32[12,256,256]{2,1,0:T(8,128)S(1)} %fusion.4, f32[256,256]{1,0:T(8,128)S(1)} %get-tuple-element.13), kind=kOutput, calls=%fused_computation.10 | convolution fusion | flops 1207959552 | bytes 6553600 | tf_op jit(solution)/shard_map/tij,kj->tik/dot_general | solution.py:16
  97.0 1.8 %collective-permute-done.18 = f32[128,256]{1,0:T(8,128)S(1)} collective-permute-done((f32[128,256]{1,0:T(8,128)S(1)}, f32[128,256]{1,0:T(8,128)S(1)}, u32[]{:S(2)}, u32[]{:S(2)}) %collective-permute-start.18) | collective-permute-done | bytes 131104 | tf_op jit(solution)/shard_map/ppermute | solution.py:23
  99.1 2.8 %fusion.8 = f32[12,256,256]{2,1,0:T(8,128)S(1)} fusion(f32[12,256,256]{2,1,0:T(8,128)S(1)} %fusion.38, f32[128,256]{1,0:T(8,128)S(1)} %add.109, f32[128,256]{1,0:T(8,128)S(1)} %add.107), kind=kOutput, calls=%fused_computation.8 | convolution fusion | flops 1208090624 | bytes 6553600 | tf_op jit(solution)/shard_map/tij,jk->tik/dot_general | solution.py:16
  101.9 1.7 %fusion.29 = f32[256,256]{1,0:T(8,128)S(1)} fusion(f32[12,256,256]{2,1,0:T(8,128)S(1)} %fusion.8, f32[12,256,256]{2,1,0:T(8,128)S(1)} %fusion.10), kind=kOutput, calls=%fused_computation.35 | convolution fusion | flops 1208025088 | bytes 6553600 | tf_op jit(solution)/shard_map/tik,tkl->il/dot_general | solution.py:16
  103.8 1.9 %collective-permute-start.23 = (f32[128,256]{1,0:T(8,128)S(1)}, f32[128,256]{1,0:T(8,128)S(1)}, u32[]{:S(2)}, u32[]{:S(2)}) collective-permute-start(f32[128,256]{1,0:T(8,128)S(1)} %get-tuple-element.20), channel_id=1, source_target_pairs={{0,6},{1,7},{2,4},{3,5},{4,2},{5,3},{6,0},{7,1},{8,14},{9,15},{10,... | collective-permute-start | bytes 393224 | tf_op jit(solution)/shard_map/ppermute | solution.py:23
  106.1 3.8 %collective-permute-done.21 = f32[128,256]{1,0:T(8,128)S(1)} collective-permute-done((f32[128,256]{1,0:T(8,128)S(1)}, f32[128,256]{1,0:T(8,128)S(1)}, u32[]{:S(2)}, u32[]{:S(2)}) %collective-permute-start.21) | collective-permute-done | bytes 131104 | tf_op jit(solution)/shard_map/ppermute | solution.py:23
  110.8 1.9 %collective-permute-start.22 = (f32[128,256]{1,0:T(8,128)S(1)}, f32[128,256]{1,0:T(8,128)S(1)}, u32[]{:S(2)}, u32[]{:S(2)}) collective-permute-start(f32[128,256]{1,0:T(8,128)S(1)} %get-tuple-element.17), channel_id=1, source_target_pairs={{0,6},{1,7},{2,4},{3,5},{4,2},{5,3},{6,0},{7,1},{8,14},{9,15},{10,... | collective-permute-start | bytes 393224 | tf_op jit(solution)/shard_map/ppermute | solution.py:23
  112.6 1.9 %collective-permute-start.24 = (f32[128,256]{1,0:T(8,128)S(1)}, f32[128,256]{1,0:T(8,128)S(1)}, u32[]{:S(2)}, u32[]{:S(2)}) collective-permute-start(f32[128,256]{1,0:T(8,128)S(1)} %get-tuple-element.18), channel_id=1, source_target_pairs={{0,1},{1,0},{2,3},{3,2},{4,5},{5,4},{6,7},{7,6},{8,9},{9,8},{10,11... | collective-permute-start | bytes 393224 | tf_op jit(solution)/shard_map/ppermute | solution.py:23
  114.8 4.2 %collective-permute-done.22 = f32[128,256]{1,0:T(8,128)S(1)} collective-permute-done((f32[128,256]{1,0:T(8,128)S(1)}, f32[128,256]{1,0:T(8,128)S(1)}, u32[]{:S(2)}, u32[]{:S(2)}) %collective-permute-start.22) | collective-permute-done | bytes 131104 | tf_op jit(solution)/shard_map/ppermute | solution.py:23
  119.1 2.0 %collective-permute-start.26 = (f32[128,256]{1,0:T(8,128)S(1)}, f32[128,256]{1,0:T(8,128)S(1)}, u32[]{:S(2)}, u32[]{:S(2)}) collective-permute-start(f32[128,256]{1,0:T(8,128)S(1)} %get-tuple-element.16), channel_id=1, source_target_pairs={{0,2},{1,3},{2,0},{3,1},{4,6},{5,7},{6,4},{7,5},{8,10},{9,11},{10,... | collective-permute-start | bytes 393224 | tf_op jit(solution)/shard_map/ppermute | solution.py:23
  121.1 2.9 %collective-permute-done.25 = f32[128,256]{1,0:T(8,128)S(1)} collective-permute-done((f32[128,256]{1,0:T(8,128)S(1)}, f32[128,256]{1,0:T(8,128)S(1)}, u32[]{:S(2)}, u32[]{:S(2)}) %collective-permute-start.25) | collective-permute-done | bytes 131104 | tf_op jit(solution)/shard_map/ppermute | solution.py:23
  124.1 1.4 %collective-permute-done.26 = f32[128,256]{1,0:T(8,128)S(1)} collective-permute-done((f32[128,256]{1,0:T(8,128)S(1)}, f32[128,256]{1,0:T(8,128)S(1)}, u32[]{:S(2)}, u32[]{:S(2)}) %collective-permute-start.26) | collective-permute-done | bytes 131104 | tf_op jit(solution)/shard_map/ppermute | solution.py:23
  (78 shorter events, 14.8 us)
Async XLA Ops:
  0.0 5.1 %copy-start = (f32[6,256,256]{2,1,0:T(8,128)S(1)}, f32[6,256,256]{2,1,0:T(8,128)}, u32[]{:S(2)}) copy-start(f32[6,256,256]{2,1,0:T(8,128)} %param.12) | copy-start | bytes 4718596
  3.6 6.2 %copy-start.3 = (s32[48,2]{0,1:T(2,128)S(1)}, s32[48,2]{0,1:T(2,128)}, u32[]{:S(2)}) copy-start(s32[48,2]{0,1:T(2,128)} %param.15) | copy-start | bytes 1156
  3.6 6.2 %copy-start.4 = (s32[6]{0:T(128)S(1)}, s32[6]{0:T(128)}, u32[]{:S(2)}) copy-start(s32[6]{0:T(128)} %param.14) | copy-start | bytes 76
  3.6 6.3 %copy-start.5 = (f32[48]{0:T(128)S(1)}, f32[48]{0:T(128)}, u32[]{:S(2)}) copy-start(f32[48]{0:T(128)} %param.13) | copy-start | bytes 580
  3.6 8.9 %copy-start.1 = (f32[6,256,256]{2,1,0:T(8,128)S(1)}, f32[6,256,256]{2,1,0:T(8,128)}, u32[]{:S(2)}) copy-start(f32[6,256,256]{2,1,0:T(8,128)} %param.11) | copy-start | bytes 4718596
  4.6 8.1 %collective-permute-start = (f32[256,256]{1,0:T(8,128)}, f32[256,256]{1,0:T(8,128)S(1)}, u32[]{:S(2)}, u32[]{:S(2)}) collective-permute-start(f32[256,256]{1,0:T(8,128)} %convolution_select_fusion), channel_id=1, source_target_pairs={{0,8},{8,0},{16,24},{24,16},{1,9},{9,1},{17,25},{25,17},{2,10},{10... | collective-permute-start | bytes 786440 | tf_op jit(solution)/shard_map/ppermute | solution.py:23
  7.2 21.2 %collective-permute-start.8 = (f32[384,256]{1,0:T(8,128)}, f32[384,256]{1,0:T(8,128)}, u32[]{:S(2)}, u32[]{:S(2)}) collective-permute-start(f32[384,256]{1,0:T(8,128)} %get-tuple-element.10), channel_id=1, source_target_pairs={{0,2},{1,3},{2,0},{3,1},{4,6},{5,7},{6,4},{7,5},{8,10},{9,11},{10,... | collective-permute-start | bytes 1179656 | tf_op jit(solution)/shard_map/ppermute | solution.py:23
  9.8 20.4 %collective-permute-start.7 = (f32[384,256]{1,0:T(8,128)}, f32[384,256]{1,0:T(8,128)}, u32[]{:S(2)}, u32[]{:S(2)}) collective-permute-start(f32[384,256]{1,0:T(8,128)} %get-tuple-element.9), channel_id=1, source_target_pairs={{0,2},{1,3},{2,0},{3,1},{4,6},{5,7},{6,4},{7,5},{8,10},{9,11},{10,... | collective-permute-start | bytes 1179656 | tf_op jit(solution)/shard_map/ppermute | solution.py:23
  10.4 17.9 %collective-permute-start.12 = (f32[6]{0:T(128)S(1)}, f32[6]{0:T(128)S(1)}, u32[]{:S(2)}, u32[]{:S(2)}) collective-permute-start(f32[6]{0:T(128)S(1)} %get-tuple-element.6), channel_id=1, source_target_pairs={{0,2},{1,3},{2,0},{3,1},{4,6},{5,7},{6,4},{7,5},{8,10},{9,11},{10,... | collective-permute-start | bytes 80 | tf_op jit(solution)/shard_map/ppermute | solution.py:23
  12.7 18.1 %copy-start.2 = (f32[1,2,256,256]{3,2,1,0:T(8,128)S(1)}, f32[1,2,256,256]{3,2,1,0:T(8,128)}, u32[]{:S(2)}) copy-start(f32[1,2,256,256]{3,2,1,0:T(8,128)} %param.8) | copy-start | bytes 1572868
  14.0 16.5 %collective-permute-start.1 = (f32[256,256]{1,0:T(8,128)S(1)}, f32[256,256]{1,0:T(8,128)S(1)}, u32[]{:S(2)}, u32[]{:S(2)}) collective-permute-start(f32[256,256]{1,0:T(8,128)S(1)} %fusion.59), channel_id=1, source_target_pairs={{0,16},{8,24},{16,0},{24,8},{1,17},{9,25},{17,1},{25,9},{2,18},{10... | collective-permute-start | bytes 786440 | tf_op jit(solution)/shard_map/ppermute | solution.py:23
  28.4 19.6 %collective-permute-start.10 = (f32[384,256]{1,0:T(8,128)}, f32[384,256]{1,0:T(8,128)S(1)}, u32[]{:S(2)}, u32[]{:S(2)}) collective-permute-start(f32[384,256]{1,0:T(8,128)} %collective-permute-done.8), channel_id=1, source_target_pairs={{0,16},{8,24},{16,0},{24,8},{1,17},{9,25},{17,1},{25,9},{2,18},{10... | collective-permute-start | bytes 1179656 | tf_op jit(solution)/shard_map/ppermute | solution.py:23
  30.1 17.9 %collective-permute-start.9 = (f32[384,256]{1,0:T(8,128)}, f32[384,256]{1,0:T(8,128)S(1)}, u32[]{:S(2)}, u32[]{:S(2)}) collective-permute-start(f32[384,256]{1,0:T(8,128)} %collective-permute-done.7), channel_id=1, source_target_pairs={{0,16},{8,24},{16,0},{24,8},{1,17},{9,25},{17,1},{25,9},{2,18},{10... | collective-permute-start | bytes 1179656 | tf_op jit(solution)/shard_map/ppermute | solution.py:23
  33.8 7.6 %collective-permute-start.2 = (f32[256,256]{1,0:T(8,128)S(1)}, f32[256,256]{1,0:T(8,128)S(1)}, u32[]{:S(2)}, u32[]{:S(2)}) collective-permute-start(f32[256,256]{1,0:T(8,128)S(1)} %fusion.23), channel_id=1, source_target_pairs={{0,2},{1,3},{2,0},{3,1},{4,6},{5,7},{6,4},{7,5},{8,10},{9,11},{10,... | collective-permute-start | bytes 786440 | tf_op jit(solution)/shard_map/ppermute | solution.py:23
  43.0 6.7 %collective-permute-start.3 = (f32[128,256]{1,0:T(8,128)S(1)}, f32[128,256]{1,0:T(8,128)S(1)}, u32[]{:S(2)}, u32[]{:S(2)}) collective-permute-start(f32[128,256]{1,0:T(8,128)S(1)} %get-tuple-element.31), channel_id=1, source_target_pairs={{0,1},{1,0},{2,3},{3,2},{4,5},{5,4},{6,7},{7,6},{8,9},{9,8},{10,11... | collective-permute-start | bytes 393224 | tf_op jit(solution)/shard_map/ppermute | solution.py:23
  44.5 6.9 %collective-permute-start.5 = (f32[128,256]{1,0:T(8,128)S(1)}, f32[128,256]{1,0:T(8,128)S(1)}, u32[]{:S(2)}, u32[]{:S(2)}) collective-permute-start(f32[128,256]{1,0:T(8,128)S(1)} %get-tuple-element.32), channel_id=1, source_target_pairs={{0,6},{1,7},{2,4},{3,5},{4,2},{5,3},{6,0},{7,1},{8,14},{9,15},{10,... | collective-permute-start | bytes 393224 | tf_op jit(solution)/shard_map/ppermute | solution.py:23
  49.3 12.9 %collective-permute-start.11 = (f32[6,256,256]{2,1,0:T(8,128)S(1)}, f32[6,256,256]{2,1,0:T(8,128)S(1)}, u32[]{:S(2)}, u32[]{:S(2)}) collective-permute-start(f32[6,256,256]{2,1,0:T(8,128)S(1)} %bitcast.134), channel_id=1, source_target_pairs={{0,8},{8,0},{16,24},{24,16},{1,9},{9,1},{17,25},{25,17},{2,10},{10... | collective-permute-start | bytes 4718600 | tf_op jit(solution)/shard_map/ppermute | solution.py:23
  51.4 6.9 %collective-permute-start.4 = (f32[128,256]{1,0:T(8,128)S(1)}, f32[128,256]{1,0:T(8,128)S(1)}, u32[]{:S(2)}, u32[]{:S(2)}) collective-permute-start(f32[128,256]{1,0:T(8,128)S(1)} %get-tuple-element.29), channel_id=1, source_target_pairs={{0,6},{1,7},{2,4},{3,5},{4,2},{5,3},{6,0},{7,1},{8,14},{9,15},{10,... | collective-permute-start | bytes 393224 | tf_op jit(solution)/shard_map/ppermute | solution.py:23
  54.9 5.0 %collective-permute-start.6 = (f32[128,256]{1,0:T(8,128)S(1)}, f32[128,256]{1,0:T(8,128)S(1)}, u32[]{:S(2)}, u32[]{:S(2)}) collective-permute-start(f32[128,256]{1,0:T(8,128)S(1)} %get-tuple-element.30), channel_id=1, source_target_pairs={{0,1},{1,0},{2,3},{3,2},{4,5},{5,4},{6,7},{7,6},{8,9},{9,8},{10,11... | collective-permute-start | bytes 393224 | tf_op jit(solution)/shard_map/ppermute | solution.py:23
  64.5 5.0 %collective-permute-start.13 = (f32[128,256]{1,0:T(8,128)S(1)}, f32[128,256]{1,0:T(8,128)S(1)}, u32[]{:S(2)}, u32[]{:S(2)}) collective-permute-start(f32[128,256]{1,0:T(8,128)S(1)} %get-tuple-element.27), channel_id=1, source_target_pairs={{0,1},{1,0},{2,3},{3,2},{4,5},{5,4},{6,7},{7,6},{8,9},{9,8},{10,11... | collective-permute-start | bytes 393224 | tf_op jit(solution)/shard_map/ppermute | solution.py:23
  65.1 6.9 %collective-permute-start.15 = (f32[128,256]{1,0:T(8,128)S(1)}, f32[128,256]{1,0:T(8,128)S(1)}, u32[]{:S(2)}, u32[]{:S(2)}) collective-permute-start(f32[128,256]{1,0:T(8,128)S(1)} %get-tuple-element.28), channel_id=1, source_target_pairs={{0,6},{1,7},{2,4},{3,5},{4,2},{5,3},{6,0},{7,1},{8,14},{9,15},{10,... | collective-permute-start | bytes 393224 | tf_op jit(solution)/shard_map/ppermute | solution.py:23
  72.0 6.9 %collective-permute-start.14 = (f32[128,256]{1,0:T(8,128)S(1)}, f32[128,256]{1,0:T(8,128)S(1)}, u32[]{:S(2)}, u32[]{:S(2)}) collective-permute-start(f32[128,256]{1,0:T(8,128)S(1)} %get-tuple-element.25), channel_id=1, source_target_pairs={{0,6},{1,7},{2,4},{3,5},{4,2},{5,3},{6,0},{7,1},{8,14},{9,15},{10,... | collective-permute-start | bytes 393224 | tf_op jit(solution)/shard_map/ppermute | solution.py:23
  74.2 5.0 %collective-permute-start.16 = (f32[128,256]{1,0:T(8,128)S(1)}, f32[128,256]{1,0:T(8,128)S(1)}, u32[]{:S(2)}, u32[]{:S(2)}) collective-permute-start(f32[128,256]{1,0:T(8,128)S(1)} %get-tuple-element.26), channel_id=1, source_target_pairs={{0,1},{1,0},{2,3},{3,2},{4,5},{5,4},{6,7},{7,6},{8,9},{9,8},{10,11... | collective-permute-start | bytes 393224 | tf_op jit(solution)/shard_map/ppermute | solution.py:23
  82.5 6.0 %collective-permute-start.17 = (f32[128,256]{1,0:T(8,128)S(1)}, f32[128,256]{1,0:T(8,128)S(1)}, u32[]{:S(2)}, u32[]{:S(2)}) collective-permute-start(f32[128,256]{1,0:T(8,128)S(1)} %get-tuple-element.23), channel_id=1, source_target_pairs={{0,1},{1,0},{2,3},{3,2},{4,5},{5,4},{6,7},{7,6},{8,9},{9,8},{10,11... | collective-permute-start | bytes 393224 | tf_op jit(solution)/shard_map/ppermute | solution.py:23
  83.8 8.2 %collective-permute-start.19 = (f32[128,256]{1,0:T(8,128)S(1)}, f32[128,256]{1,0:T(8,128)S(1)}, u32[]{:S(2)}, u32[]{:S(2)}) collective-permute-start(f32[128,256]{1,0:T(8,128)S(1)} %get-tuple-element.24), channel_id=1, source_target_pairs={{0,6},{1,7},{2,4},{3,5},{4,2},{5,3},{6,0},{7,1},{8,14},{9,15},{10,... | collective-permute-start | bytes 393224 | tf_op jit(solution)/shard_map/ppermute | solution.py:23
  92.0 6.8 %collective-permute-start.18 = (f32[128,256]{1,0:T(8,128)S(1)}, f32[128,256]{1,0:T(8,128)S(1)}, u32[]{:S(2)}, u32[]{:S(2)}) collective-permute-start(f32[128,256]{1,0:T(8,128)S(1)} %get-tuple-element.21), channel_id=1, source_target_pairs={{0,6},{1,7},{2,4},{3,5},{4,2},{5,3},{6,0},{7,1},{8,14},{9,15},{10,... | collective-permute-start | bytes 393224 | tf_op jit(solution)/shard_map/ppermute | solution.py:23
  94.1 5.0 %collective-permute-start.20 = (f32[128,256]{1,0:T(8,128)S(1)}, f32[128,256]{1,0:T(8,128)S(1)}, u32[]{:S(2)}, u32[]{:S(2)}) collective-permute-start(f32[128,256]{1,0:T(8,128)S(1)} %get-tuple-element.22), channel_id=1, source_target_pairs={{0,1},{1,0},{2,3},{3,2},{4,5},{5,4},{6,7},{7,6},{8,9},{9,8},{10,11... | collective-permute-start | bytes 393224 | tf_op jit(solution)/shard_map/ppermute | solution.py:23
  103.6 6.3 %collective-permute-start.21 = (f32[128,256]{1,0:T(8,128)S(1)}, f32[128,256]{1,0:T(8,128)S(1)}, u32[]{:S(2)}, u32[]{:S(2)}) collective-permute-start(f32[128,256]{1,0:T(8,128)S(1)} %get-tuple-element.19), channel_id=1, source_target_pairs={{0,1},{1,0},{2,3},{3,2},{4,5},{5,4},{6,7},{7,6},{8,9},{9,8},{10,11... | collective-permute-start | bytes 393224 | tf_op jit(solution)/shard_map/ppermute | solution.py:23
  103.8 6.9 %collective-permute-start.23 = (f32[128,256]{1,0:T(8,128)S(1)}, f32[128,256]{1,0:T(8,128)S(1)}, u32[]{:S(2)}, u32[]{:S(2)}) collective-permute-start(f32[128,256]{1,0:T(8,128)S(1)} %get-tuple-element.20), channel_id=1, source_target_pairs={{0,6},{1,7},{2,4},{3,5},{4,2},{5,3},{6,0},{7,1},{8,14},{9,15},{10,... | collective-permute-start | bytes 393224 | tf_op jit(solution)/shard_map/ppermute | solution.py:23
  110.8 8.2 %collective-permute-start.22 = (f32[128,256]{1,0:T(8,128)S(1)}, f32[128,256]{1,0:T(8,128)S(1)}, u32[]{:S(2)}, u32[]{:S(2)}) collective-permute-start(f32[128,256]{1,0:T(8,128)S(1)} %get-tuple-element.17), channel_id=1, source_target_pairs={{0,6},{1,7},{2,4},{3,5},{4,2},{5,3},{6,0},{7,1},{8,14},{9,15},{10,... | collective-permute-start | bytes 393224 | tf_op jit(solution)/shard_map/ppermute | solution.py:23
  112.6 6.4 %collective-permute-start.24 = (f32[128,256]{1,0:T(8,128)S(1)}, f32[128,256]{1,0:T(8,128)S(1)}, u32[]{:S(2)}, u32[]{:S(2)}) collective-permute-start(f32[128,256]{1,0:T(8,128)S(1)} %get-tuple-element.18), channel_id=1, source_target_pairs={{0,1},{1,0},{2,3},{3,2},{4,5},{5,4},{6,7},{7,6},{8,9},{9,8},{10,11... | collective-permute-start | bytes 393224 | tf_op jit(solution)/shard_map/ppermute | solution.py:23
  119.0 5.0 %collective-permute-start.25 = (f32[128,256]{1,0:T(8,128)S(1)}, f32[128,256]{1,0:T(8,128)S(1)}, u32[]{:S(2)}, u32[]{:S(2)}) collective-permute-start(f32[128,256]{1,0:T(8,128)S(1)} %get-tuple-element.15), channel_id=1, source_target_pairs={{0,2},{1,3},{2,0},{3,1},{4,6},{5,7},{6,4},{7,5},{8,10},{9,11},{10,... | collective-permute-start | bytes 393224 | tf_op jit(solution)/shard_map/ppermute | solution.py:23
  119.1 6.3 %collective-permute-start.26 = (f32[128,256]{1,0:T(8,128)S(1)}, f32[128,256]{1,0:T(8,128)S(1)}, u32[]{:S(2)}, u32[]{:S(2)}) collective-permute-start(f32[128,256]{1,0:T(8,128)S(1)} %get-tuple-element.16), channel_id=1, source_target_pairs={{0,2},{1,3},{2,0},{3,1},{4,6},{5,7},{6,4},{7,5},{8,10},{9,11},{10,... | collective-permute-start | bytes 393224 | tf_op jit(solution)/shard_map/ppermute | solution.py:23

commit v2 on v1

--- a/solution.py
+++ b/solution.py
@@ -79,16 +79,20 @@
 def sum_groups(partial):
     masks = sum_masks()
     half = partial.shape[0] // 2
-    upper, lower = partial[:half], partial[half:]
+    upper = lax.optimization_barrier(partial[:half])
+    lower = lax.optimization_barrier(partial[half:])
     for i in range(len(masks)):
-        upper, lower = (
-            upper + swap(upper, "term", masks[i]), lower + swap(lower, "term", masks[-1 - i])
-        )
+        from_upper = swap(upper, "term", masks[i])
+        from_lower = swap(lower, "term", masks[-1 - i])
+        upper, lower = upper + from_upper, lower + from_lower
     return upper, lower
 
 
-def apply_terms(tensor, lefts, rights):
-    return contract("tik,tkl->il", contract("tij,jk->tik", lefts, tensor), rights)
+def apply_terms(tensor, lefts, rights, weights=None):
+    lefted = contract("tij,jk->tik", lefts, tensor)
+    if weights is not None:
+        lefted = lax.optimization_barrier(lefted * weights[:, None, None])
+    return contract("tik,tkl->il", lefted, rights)
 
 
 def on_device(
@@ -97,7 +101,6 @@
     width = center.shape[2]
     slots = left_edge.shape[0]
     half = slots // 2
-    piece = half * width // 2
     place = lax.axis_index("term")
     mine = ((place >> 1) ^ (place >> 2)) & 1
     spot = lax.axis_index("sec")
@@ -112,24 +115,24 @@
     keep_weight = jnp.where(mine == 0, weight[:, 0], weight[:, 1])
     give_weight = jnp.where(mine == 0, weight[:, 1], weight[:, 0])
 
-    flat_left = left_edge.reshape(slots * width, width)
-    flat_right = right_edge.reshape(slots * width, width)
-    pieces = []
-    for i in range(2):
-        start = side * (half * width) + i * piece
-        cut = jnp.where(
-            core == 0,
-            lax.dynamic_slice_in_dim(flat_left, start, piece, 0),
-            lax.dynamic_slice_in_dim(flat_right, start, piece, 0),
-        )
-        pieces.append(swap(cut, "term", PAIR))
-    shared = [swap(pieces[i], "sec", 2) for i in range(2)]
-    halves = jnp.concatenate(pieces + shared, axis=0).reshape(slots, width, width)
-    traded = swap(halves, "sec", 1)
+    rows = slots * width // 4
+    place_in_four = (2 * side + core) * rows
+    ends = []
+    cuts = [
+        lax.dynamic_slice_in_dim(edge.reshape(-1, width), place_in_four, rows, 0)
+        for edge in (left_edge, right_edge)
+    ]
+    site_maps, *cuts = lax.optimization_barrier([site_maps] + cuts)
+    for cut in cuts:
+        near = swap(cut, "term", PAIR)
+        far = swap(near, "sec", 2)
+        held = jnp.stack([near, far])
+        traded = swap(held, "sec", 1)
+        held, traded = jnp.where(core == 0, held, traded), jnp.where(core == 0, traded, held)
+        ends.append(jnp.stack([held, traded], axis=1).reshape(slots, width, width))
+    other_left, other_right = ends
     others = swap(give_weight, "term", PAIR)
     others = jnp.where(side == 0, others, jnp.roll(others, half))
-    other_left = jnp.where(core == 0, halves, traded) * others[:, None, None]
-    other_right = jnp.where(core == 0, traded, halves)
 
     section_map = section_product(site_maps, section_sites[0])
     prefix, suffix = scan_maps(section_map)
@@ -140,8 +143,7 @@
 
     def first(start, weights):
         turned = product(product(prefix, start), suffix)
-        lefted = contract("tij,jk->tik", left_edge, turned) * weights[:, None, None]
-        return contract("tik,tkl->il", lefted, right_edge)
+        return apply_terms(turned, left_edge, right_edge, weights)
 
     given = first(start_give, give_weight)
     kept = first(start_keep, keep_weight)
@@ -151,20 +153,18 @@
 
     gram_left = contract("ij,kj->ik", prefix, prefix)
     gram_right = contract("ji,jk->ik", suffix, suffix)
-    own_left = left_edge * keep_weight[:, None, None]
 
     turned = product(product(gram_left, current), gram_right)
-    partial = apply_terms(turned, own_left, right_edge)
-    partial = partial + apply_terms(turned, other_left, other_right)
+    partial = apply_terms(turned, left_edge, right_edge, keep_weight)
+    partial = partial + apply_terms(turned, other_left, other_right, others)
     current = jnp.concatenate(sum_groups(partial), axis=0) * (-TAYLOR_STEP / 2)
     total = total + current
 
-    lefts = jnp.concatenate([own_left, other_left], axis=0)
+    weights = jnp.concatenate([keep_weight, others])
+    lefts = jnp.concatenate([left_edge, other_left], axis=0)
     rights = jnp.concatenate([right_edge, other_right], axis=0)
-    lefts = contract("tij,jk->tik", lefts, gram_left)
+    lefts = contract("tij,jk->tik", lefts, gram_left) * weights[:, None, None]
     rights = contract("ij,tjk->tik", gram_right, rights)
-    lefts_out = contract("ji,tjk->tik", prefix, lefts)
-    rights_out = contract("tij,kj->tik", rights, suffix)
 
     for order in range(3, ORDER):
         partial = apply_terms(current, lefts, rights)
@@ -172,7 +172,8 @@
         current = current * (-TAYLOR_STEP / order)
         total = total + current
 
-    partial = apply_terms(current, lefts_out, rights_out) * (-TAYLOR_STEP / ORDER)
+    partial = apply_terms(current, lefts, rights) * (-TAYLOR_STEP / ORDER)
+    partial = contract("ij,kj->ik", contract("ji,jk->ik", prefix, partial), suffix)
     so_far = start_keep + contract("ij,kj->ik", contract("ji,jk->ik", prefix, total), suffix)
     ends = sum_groups(partial)
     ours, theirs = [], []

time: 127 us -> 124 us (0.976)
  matrix products: 34.4 us -> 25.7 us
  waiting for transfers between devices: 45.5 us -> 50.4 us
  other arithmetic: 5.7 us -> 2.47 us
  starting transfers between devices: 39.3 us -> 42.3 us
  local copies, waits for them, and re-layouts: 0.18 us -> 1.99 us
    ppermute x27 -> x28, waiting for transfers between devices: 45.5 us -> 50.4 us  [swap(): return lax.ppermute(value, axis, pairs)]
    dot_general x20, matrix products: 27.1 us -> 22.4 us  [contract(): jnp.einsum(spec, left, right, precision=lax.Precision.HIGH, preferred_ele...]
    dot_general x11, matrix products: 7.25 us -> 3.32 us  [product(): jnp.dot(left, right, precision=lax.Precision.HIGH, preferred_element_type...]
    ppermute x27 -> x28, starting transfers between devices: 39.3 us -> 42.3 us  [swap(): return lax.ppermute(value, axis, pairs)]
    select_n x2 -> x0, other arithmetic: 2.45 us -> none  [the longest x1 2.08 us: on_device(): jnp.where(core == 0, lax.dynamic_slice_in_dim(flat_left, start, piece, 0)...]
  transfers between devices with their start and end apart: 27 -> 28, of which waited for: 17 -> 17; matrix products, arithmetic and copies ran while one was open for 20% -> 14% of each run, Pallas kernels for 0% -> 0%
where the time goes in v2:
time: 124 us
  waiting for transfers between devices  50.4 us (41%)
  starting transfers between devices  42.3 us (34%)
  matrix products  25.7 us (21%)
  other arithmetic  2.47 us (2%)
  local copies, waits for them, and re-layouts  1.99 us (2%)
  between operations  1.25 us (1%)
    ppermute x28, waiting for transfers between devices, swap(): return lax.ppermute(value, axis, pairs)  50.4 us
    ppermute x28, starting transfers between devices, swap(): return lax.ppermute(value, axis, pairs)  42.3 us
    dot_general x20, matrix products, contract(): jnp.einsum(spec, left, right, precision=lax.Precision.HIGH, preferred_ele...  22.4 us
    dot_general x11, matrix products, product(): jnp.dot(left, right, precision=lax.Precision.HIGH, preferred_element_type...  3.32 us
  transfers between devices with their start and end apart: 28, of which 17 were waited for; matrix products, arithmetic and copies ran while one was open for 14% of the time, Pallas kernels for 0%

profile of v2, /device:TPU:0, one launch (start us, length us, event | category | flops | bytes accessed | tf_op | source)
XLA Modules:
  0.0 124.1 jit_solution(2616402151445033923)
XLA Ops:
  0.7 1.2 constant_dynamic-slice_fusion
  4.0 2.6 %collective-permute-start.10 = (f32[6]{0:T(128)S(1)}, f32[6]{0:T(128)S(1)}, u32[]{:S(2)}, u32[]{:S(2)}) collective-permute-start(f32[6]{0:T(128)S(1)} %get-tuple-element.12), channel_id=1, source_target_pairs={{0,2},{1,3},{2,0},{3,1},{4,6},{5,7},{6,4},{7,5},{8,10},{9,11},{10,... | collective-permute-start | bytes 80 | tf_op jit(solution)/shard_map/ppermute | solution.py:23
  6.7 1.9 %collective-permute-start.11 = (f32[384,256]{1,0:T(8,128)S(1)}, f32[384,256]{1,0:T(8,128)S(1)}, u32[]{:S(2)}, u32[]{:S(2)}) collective-permute-start(f32[384,256]{1,0:T(8,128)S(1)} %get-tuple-element.10), channel_id=1, source_target_pairs={{0,2},{1,3},{2,0},{3,1},{4,6},{5,7},{6,4},{7,5},{8,10},{9,11},{10,... | collective-permute-start | bytes 1179656 | tf_op jit(solution)/shard_map/ppermute | solution.py:23
  9.0 1.6 %collective-permute-start.1 = (f32[256,256]{1,0:T(8,128)S(1)}, f32[256,256]{1,0:T(8,128)S(1)}, u32[]{:S(2)}, u32[]{:S(2)}) collective-permute-start(f32[256,256]{1,0:T(8,128)S(1)} %fusion.48), channel_id=1, source_target_pairs={{0,16},{8,24},{16,0},{24,8},{1,17},{9,25},{17,1},{25,9},{2,18},{10... | collective-permute-start | bytes 786440 | tf_op jit(solution)/shard_map/ppermute | solution.py:23
  10.8 7.9 %collective-permute-done.7 = f32[384,256]{1,0:T(8,128)S(1)} collective-permute-done((f32[384,256]{1,0:T(8,128)S(1)}, f32[384,256]{1,0:T(8,128)S(1)}, u32[]{:S(2)}, u32[]{:S(2)}) %collective-permute-start.7) | collective-permute-done | bytes 393248 | tf_op jit(solution)/shard_map/ppermute | solution.py:23
  18.6 1.5 %collective-permute-start.8 = (f32[384,256]{1,0:T(8,128)S(1)}, f32[384,256]{1,0:T(8,128)S(1)}, u32[]{:S(2)}, u32[]{:S(2)}) collective-permute-start(f32[384,256]{1,0:T(8,128)S(1)} %collective-permute-done.7), channel_id=1, source_target_pairs={{0,16},{8,24},{16,0},{24,8},{1,17},{9,25},{17,1},{25,9},{2,18},{10... | collective-permute-start | bytes 1179656 | tf_op jit(solution)/shard_map/ppermute | solution.py:23
  20.2 6.1 %collective-permute-done.11 = f32[384,256]{1,0:T(8,128)S(1)} collective-permute-done((f32[384,256]{1,0:T(8,128)S(1)}, f32[384,256]{1,0:T(8,128)S(1)}, u32[]{:S(2)}, u32[]{:S(2)}) %collective-permute-start.11) | collective-permute-done | bytes 393248 | tf_op jit(solution)/shard_map/ppermute | solution.py:23
  26.3 1.5 %collective-permute-start.12 = (f32[384,256]{1,0:T(8,128)S(1)}, f32[384,256]{1,0:T(8,128)S(1)}, u32[]{:S(2)}, u32[]{:S(2)}) collective-permute-start(f32[384,256]{1,0:T(8,128)S(1)} %collective-permute-done.11), channel_id=1, source_target_pairs={{0,16},{8,24},{16,0},{24,8},{1,17},{9,25},{17,1},{25,9},{2,18},{10... | collective-permute-start | bytes 1179656 | tf_op jit(solution)/shard_map/ppermute | solution.py:23
  29.6 0.9 multiply_bitcast_fusion.1
  31.0 1.5 %convolution_bitcast_fusion.3 = f32[256,256]{1,0:T(8,128)S(1)} fusion(f32[6,256,256]{1,2,0:T(8,128)S(1)} %multiply_bitcast_fusion.1, f32[6,256,256]{2,1,0:T(8,128)S(1)} %copy-done), kind=kOutput, calls=%fused_computation.30 | convolution fusion | flops 603979776 | bytes 3407872 | tf_op jit(solution)/shard_map/tik,tkl->il/dot_general | solution.py:16
  33.0 0.9 multiply_bitcast_fusion.2
  34.6 5.2 %collective-permute-done.2 = f32[256,256]{1,0:T(8,128)S(1)} collective-permute-done((f32[256,256]{1,0:T(8,128)S(1)}, f32[256,256]{1,0:T(8,128)S(1)}, u32[]{:S(2)}, u32[]{:S(2)}) %collective-permute-start.2) | collective-permute-done | bytes 262176 | tf_op jit(solution)/shard_map/ppermute | solution.py:23
  39.8 1.5 %fusion.27 = f32[256,256]{1,0:T(8,128)S(1)} fusion(f32[256,256]{1,0:T(8,128)S(1)} %collective-permute-done.2, f32[6,256,256]{1,2,0:T(8,128)S(1)} %multiply_bitcast_fusion.2, f32[6,256,256]{2,1,0:T(8,128)S(1)} %copy-done), kind=kOutput, calls=%fused_computation.37 | convolution fusion | flops 604045312 | bytes 3670016 | tf_op jit(solution)/shard_map/tik,tkl->il/dot_general | solution.py:16
  41.3 2.6 %collective-permute-start.5 = (f32[128,256]{1,0:T(8,128)S(1)}, f32[128,256]{1,0:T(8,128)S(1)}, u32[]{:S(2)}, u32[]{:S(2)}) collective-permute-start(f32[128,256]{1,0:T(8,128)S(1)} %get-tuple-element.30), channel_id=1, source_target_pairs={{0,6},{1,7},{2,4},{3,5},{4,2},{5,3},{6,0},{7,1},{8,14},{9,15},{10,... | collective-permute-start | bytes 393224 | tf_op jit(solution)/shard_map/ppermute | solution.py:23
  43.9 1.5 %collective-permute-start.3 = (f32[128,256]{1,0:T(8,128)S(1)}, f32[128,256]{1,0:T(8,128)S(1)}, u32[]{:S(2)}, u32[]{:S(2)}) collective-permute-start(f32[128,256]{1,0:T(8,128)S(1)} %get-tuple-element.29), channel_id=1, source_target_pairs={{0,1},{1,0},{2,3},{3,2},{4,5},{5,4},{6,7},{7,6},{8,9},{9,8},{10,11... | collective-permute-start | bytes 393224 | tf_op jit(solution)/shard_map/ppermute | solution.py:23
  45.5 2.8 %collective-permute-done.5 = f32[128,256]{1,0:T(8,128)S(1)} collective-permute-done((f32[128,256]{1,0:T(8,128)S(1)}, f32[128,256]{1,0:T(8,128)S(1)}, u32[]{:S(2)}, u32[]{:S(2)}) %collective-permute-start.5) | collective-permute-done | bytes 131104 | tf_op jit(solution)/shard_map/ppermute | solution.py:23
  48.3 1.6 %collective-permute-start.6 = (f32[128,256]{1,0:T(8,128)S(1)}, f32[128,256]{1,0:T(8,128)S(1)}, u32[]{:S(2)}, u32[]{:S(2)}) collective-permute-start(f32[128,256]{1,0:T(8,128)S(1)} %add.91), channel_id=1, source_target_pairs={{0,1},{1,0},{2,3},{3,2},{4,5},{5,4},{6,7},{7,6},{8,9},{9,8},{10,11... | collective-permute-start | bytes 393224 | tf_op jit(solution)/shard_map/ppermute | solution.py:23
  49.9 2.6 %collective-permute-start.4 = (f32[128,256]{1,0:T(8,128)S(1)}, f32[128,256]{1,0:T(8,128)S(1)}, u32[]{:S(2)}, u32[]{:S(2)}) collective-permute-start(f32[128,256]{1,0:T(8,128)S(1)} %add.89), channel_id=1, source_target_pairs={{0,6},{1,7},{2,4},{3,5},{4,2},{5,3},{6,0},{7,1},{8,14},{9,15},{10,... | collective-permute-start | bytes 393224 | tf_op jit(solution)/shard_map/ppermute | solution.py:23
  53.4 3.4 %collective-permute-done.4 = f32[128,256]{1,0:T(8,128)S(1)} collective-permute-done((f32[128,256]{1,0:T(8,128)S(1)}, f32[128,256]{1,0:T(8,128)S(1)}, u32[]{:S(2)}, u32[]{:S(2)}) %collective-permute-start.4) | collective-permute-done | bytes 131104 | tf_op jit(solution)/shard_map/ppermute | solution.py:23
  57.3 1.6 %multiply_bitcast_fusion = f32[6,256,256]{1,2,0:T(8,128)S(1)} fusion(f32[256,256,1]{1,0,2:T(8,128)S(1)} %convolution_bitcast_fusion.2, f32[6,256,256]{2,1,0:T(8,128)S(1)} %copy-done.1, f32[6]{0:T(128)S(1)} %get-tuple-element.11), kind=kOutput, calls=%fused_computation.20 | convolution fusion | flops 604372992 | bytes 3407896 | tf_op jit(solution)/shard_map/tij,jk->tik/dot_general | solution.py:16
  58.9 1.7 %convolution_bitcast_fusion.1 = f32[256,256]{1,0:T(8,128)S(1)} fusion(f32[6,256,256]{1,2,0:T(8,128)S(1)} %multiply_bitcast_fusion, f32[6,256,256]{2,1,0:T(8,128)S(1)} %copy-done), kind=kOutput, calls=%fused_computation.28 | convolution fusion | flops 603979776 | bytes 3407872 | tf_op jit(solution)/shard_map/tik,tkl->il/dot_general | solution.py:16
  62.0 0.9 fusion.28
  63.0 2.6 %collective-permute-start.16 = (f32[128,256]{1,0:T(8,128)S(1)}, f32[128,256]{1,0:T(8,128)S(1)}, u32[]{:S(2)}, u32[]{:S(2)}) collective-permute-start(f32[128,256]{1,0:T(8,128)S(1)} %get-tuple-element.28), channel_id=1, source_target_pairs={{0,6},{1,7},{2,4},{3,5},{4,2},{5,3},{6,0},{7,1},{8,14},{9,15},{10,... | collective-permute-start | bytes 393224 | tf_op jit(solution)/shard_map/ppermute | solution.py:23
  66.2 2.7 %fusion.4 = f32[12,256,256]{2,1,0:T(8,128)S(1)} fusion(f32[6,256,256]{2,1,0:T(8,128)S(1)} %bitcast.145, f32[6,256,256]{2,1,0:T(8,128)S(1)} %copy-done, f32[256,256]{1,0:T(8,128)S(1)} %fusion.90), kind=kOutput, calls=%fused_computation.4 | convolution fusion | flops 1208745984 | bytes 6553600 | tf_op jit(solution)/shard_map/ij,tjk->tik/dot_general | solution.py:16
  68.9 1.0 collective-permute-done.16
  69.9 1.4 %collective-permute-start.17 = (f32[128,256]{1,0:T(8,128)S(1)}, f32[128,256]{1,0:T(8,128)S(1)}, u32[]{:S(2)}, u32[]{:S(2)}) collective-permute-start(f32[128,256]{1,0:T(8,128)S(1)} %add.96), channel_id=1, source_target_pairs={{0,1},{1,0},{2,3},{3,2},{4,5},{5,4},{6,7},{7,6},{8,9},{9,8},{10,11... | collective-permute-start | bytes 393224 | tf_op jit(solution)/shard_map/ppermute | solution.py:23
  71.4 1.8 %collective-permute-start.15 = (f32[128,256]{1,0:T(8,128)S(1)}, f32[128,256]{1,0:T(8,128)S(1)}, u32[]{:S(2)}, u32[]{:S(2)}) collective-permute-start(f32[128,256]{1,0:T(8,128)S(1)} %add.94), channel_id=1, source_target_pairs={{0,6},{1,7},{2,4},{3,5},{4,2},{5,3},{6,0},{7,1},{8,14},{9,15},{10,... | collective-permute-start | bytes 393224 | tf_op jit(solution)/shard_map/ppermute | solution.py:23
  73.2 1.4 %fusion = f32[12,256,256]{2,1,0:T(8,128)S(1)} fusion(f32[6,256,256]{2,1,0:T(8,128)S(1)} %bitcast.143, f32[6,256,256]{2,1,0:T(8,128)S(1)} %copy-done.1, f32[256,256]{1,0:T(8,128)S(1)} %fusion.89), kind=kOutput, calls=%fused_computation | convolution fusion | flops 1208745984 | bytes 6553600 | tf_op jit(solution)/shard_map/tij,jk->tik/dot_general | solution.py:16
  75.0 3.2 %collective-permute-done.15 = f32[128,256]{1,0:T(8,128)S(1)} collective-permute-done((f32[128,256]{1,0:T(8,128)S(1)}, f32[128,256]{1,0:T(8,128)S(1)}, u32[]{:S(2)}, u32[]{:S(2)}) %collective-permute-start.15) | collective-permute-done | bytes 131104 | tf_op jit(solution)/shard_map/ppermute | solution.py:23
  78.2 1.4 %fusion.14 = f32[12,256,256]{2,1,0:T(8,128)S(1)} fusion(f32[12,256,256]{2,1,0:T(8,128)S(1)} %fusion, f32[12]{0:T(128)S(1)} %pad_maximum_fusion.6, f32[128,256]{1,0:T(8,128)S(1)} %add.97, f32[128,256]{1,0:T(8,128)S(1)} %add.95), kind=kOutput, calls=%fused_computation.14 | convolution fusion | flops 1208877056 | bytes 6553648 | tf_op jit(solution)/shard_map/tij,jk->tik/dot_general | solution.py:16
  79.7 1.6 %fusion.18 = f32[256,256]{1,0:T(8,128)S(1)} fusion(f32[12,256,256]{2,1,0:T(8,128)S(1)} %fusion.14, f32[12,256,256]{2,1,0:T(8,128)S(1)} %fusion.4), kind=kOutput, calls=%fused_computation.34 | convolution fusion | flops 1207959552 | bytes 6553600 | tf_op jit(solution)/shard_map/tik,tkl->il/dot_general | solution.py:16
  81.3 1.9 %collective-permute-start.20 = (f32[128,256]{1,0:T(8,128)S(1)}, f32[128,256]{1,0:T(8,128)S(1)}, u32[]{:S(2)}, u32[]{:S(2)}) collective-permute-start(f32[128,256]{1,0:T(8,128)S(1)} %get-tuple-element.26), channel_id=1, source_target_pairs={{0,6},{1,7},{2,4},{3,5},{4,2},{5,3},{6,0},{7,1},{8,14},{9,15},{10,... | collective-permute-start | bytes 393224 | tf_op jit(solution)/shard_map/ppermute | solution.py:23
  83.2 1.9 %collective-permute-start.18 = (f32[128,256]{1,0:T(8,128)S(1)}, f32[128,256]{1,0:T(8,128)S(1)}, u32[]{:S(2)}, u32[]{:S(2)}) collective-permute-start(f32[128,256]{1,0:T(8,128)S(1)} %get-tuple-element.25), channel_id=1, source_target_pairs={{0,1},{1,0},{2,3},{3,2},{4,5},{5,4},{6,7},{7,6},{8,9},{9,8},{10,11... | collective-permute-start | bytes 393224 | tf_op jit(solution)/shard_map/ppermute | solution.py:23
  85.1 3.5 %collective-permute-done.20 = f32[128,256]{1,0:T(8,128)S(1)} collective-permute-done((f32[128,256]{1,0:T(8,128)S(1)}, f32[128,256]{1,0:T(8,128)S(1)}, u32[]{:S(2)}, u32[]{:S(2)}) %collective-permute-start.20) | collective-permute-done | bytes 131104 | tf_op jit(solution)/shard_map/ppermute | solution.py:23
  89.4 2.7 %collective-permute-start.19 = (f32[128,256]{1,0:T(8,128)S(1)}, f32[128,256]{1,0:T(8,128)S(1)}, u32[]{:S(2)}, u32[]{:S(2)}) collective-permute-start(f32[128,256]{1,0:T(8,128)S(1)} %add.99), channel_id=1, source_target_pairs={{0,6},{1,7},{2,4},{3,5},{4,2},{5,3},{6,0},{7,1},{8,14},{9,15},{10,... | collective-permute-start | bytes 393224 | tf_op jit(solution)/shard_map/ppermute | solution.py:23
  92.1 1.7 %collective-permute-done.21 = f32[128,256]{1,0:T(8,128)S(1)} collective-permute-done((f32[128,256]{1,0:T(8,128)S(1)}, f32[128,256]{1,0:T(8,128)S(1)}, u32[]{:S(2)}, u32[]{:S(2)}) %collective-permute-start.21) | collective-permute-done | bytes 131104 | tf_op jit(solution)/shard_map/ppermute | solution.py:23
  93.7 2.5 %collective-permute-done.19 = f32[128,256]{1,0:T(8,128)S(1)} collective-permute-done((f32[128,256]{1,0:T(8,128)S(1)}, f32[128,256]{1,0:T(8,128)S(1)}, u32[]{:S(2)}, u32[]{:S(2)}) %collective-permute-start.19) | collective-permute-done | bytes 131104 | tf_op jit(solution)/shard_map/ppermute | solution.py:23
  96.3 1.4 %fusion.12 = f32[12,256,256]{2,1,0:T(8,128)S(1)} fusion(f32[12,256,256]{2,1,0:T(8,128)S(1)} %fusion, f32[12]{0:T(128)S(1)} %pad_maximum_fusion.6, f32[128,256]{1,0:T(8,128)S(1)} %add.102, f32[128,256]{1,0:T(8,128)S(1)} %add.100), kind=kOutput, calls=%fused_computation.12 | convolution fusion | flops 1208877056 | bytes 6553648 | tf_op jit(solution)/shard_map/tij,jk->tik/dot_general | solution.py:16
  97.8 1.8 %fusion.24 = f32[256,256]{1,0:T(8,128)S(1)} fusion(f32[12,256,256]{2,1,0:T(8,128)S(1)} %fusion.12, f32[12,256,256]{2,1,0:T(8,128)S(1)} %fusion.4), kind=kOutput, calls=%fused_computation.36 | convolution fusion | flops 1208025088 | bytes 6553600 | tf_op jit(solution)/shard_map/tik,tkl->il/dot_general | solution.py:16
  100.4 3.5 %collective-permute-start.24 = (f32[128,256]{1,0:T(8,128)S(1)}, f32[128,256]{1,0:T(8,128)S(1)}, u32[]{:S(2)}, u32[]{:S(2)}) collective-permute-start(f32[128,256]{1,0:T(8,128)S(1)} %get-tuple-element.24), channel_id=1, source_target_pairs={{0,6},{1,7},{2,4},{3,5},{4,2},{5,3},{6,0},{7,1},{8,14},{9,15},{10,... | collective-permute-start | bytes 393224 | tf_op jit(solution)/shard_map/ppermute | solution.py:23
  104.8 2.5 %collective-permute-done.24 = f32[128,256]{1,0:T(8,128)S(1)} collective-permute-done((f32[128,256]{1,0:T(8,128)S(1)}, f32[128,256]{1,0:T(8,128)S(1)}, u32[]{:S(2)}, u32[]{:S(2)}) %collective-permute-start.24) | collective-permute-done | bytes 131104 | tf_op jit(solution)/shard_map/ppermute | solution.py:23
  107.3 2.4 %collective-permute-start.25 = (f32[128,256]{1,0:T(8,128)S(1)}, f32[128,256]{1,0:T(8,128)S(1)}, u32[]{:S(2)}, u32[]{:S(2)}) collective-permute-start(f32[128,256]{1,0:T(8,128)S(1)} %add.108), channel_id=1, source_target_pairs={{0,1},{1,0},{2,3},{3,2},{4,5},{5,4},{6,7},{7,6},{8,9},{9,8},{10,11... | collective-permute-start | bytes 393224 | tf_op jit(solution)/shard_map/ppermute | solution.py:23
  109.8 1.6 %collective-permute-start.23 = (f32[128,256]{1,0:T(8,128)S(1)}, f32[128,256]{1,0:T(8,128)S(1)}, u32[]{:S(2)}, u32[]{:S(2)}) collective-permute-start(f32[128,256]{1,0:T(8,128)S(1)} %add.105), channel_id=1, source_target_pairs={{0,6},{1,7},{2,4},{3,5},{4,2},{5,3},{6,0},{7,1},{8,14},{9,15},{10,... | collective-permute-start | bytes 393224 | tf_op jit(solution)/shard_map/ppermute | solution.py:23
  111.7 1.0 collective-permute-done.25
  112.7 4.0 %collective-permute-done.23 = f32[128,256]{1,0:T(8,128)S(1)} collective-permute-done((f32[128,256]{1,0:T(8,128)S(1)}, f32[128,256]{1,0:T(8,128)S(1)}, u32[]{:S(2)}, u32[]{:S(2)}) %collective-permute-start.23) | collective-permute-done | bytes 131104 | tf_op jit(solution)/shard_map/ppermute | solution.py:23
  116.8 1.5 %collective-permute-start.26 = (f32[128,256]{1,0:T(8,128)S(1)}, f32[128,256]{1,0:T(8,128)S(1)}, u32[]{:S(2)}, u32[]{:S(2)}) collective-permute-start(f32[128,256]{1,0:T(8,128)S(1)} %get-tuple-element.21), channel_id=1, source_target_pairs={{0,2},{1,3},{2,0},{3,1},{4,6},{5,7},{6,4},{7,5},{8,10},{9,11},{10,... | collective-permute-start | bytes 393224 | tf_op jit(solution)/shard_map/ppermute | solution.py:23
  118.9 2.9 %collective-permute-done.26 = f32[128,256]{1,0:T(8,128)S(1)} collective-permute-done((f32[128,256]{1,0:T(8,128)S(1)}, f32[128,256]{1,0:T(8,128)S(1)}, u32[]{:S(2)}, u32[]{:S(2)}) %collective-permute-start.26) | collective-permute-done | bytes 131104 | tf_op jit(solution)/shard_map/ppermute | solution.py:23
  121.8 1.5 %collective-permute-done.27 = f32[128,256]{1,0:T(8,128)S(1)} collective-permute-done((f32[128,256]{1,0:T(8,128)S(1)}, f32[128,256]{1,0:T(8,128)S(1)}, u32[]{:S(2)}, u32[]{:S(2)}) %collective-permute-start.27) | collective-permute-done | bytes 131104 | tf_op jit(solution)/shard_map/ppermute | solution.py:23
  (91 shorter events, 14.3 us)
Async XLA Ops:
  0.0 2.0 %copy-start.3 = (f32[4,256,256]{2,1,0:T(8,128)S(1)}, f32[4,256,256]{2,1,0:T(8,128)}, u32[]{:S(2)}) copy-start(f32[4,256,256]{2,1,0:T(8,128)} %param.9) | copy-start | bytes 3145732
  1.9 1.5 %copy-start.5 = (s32[6]{0:T(128)S(1)}, s32[6]{0:T(128)}, u32[]{:S(2)}) copy-start(s32[6]{0:T(128)} %param.14) | copy-start | bytes 76
  1.9 1.5 %copy-start.6 = (f32[48]{0:T(128)S(1)}, f32[48]{0:T(128)}, u32[]{:S(2)}) copy-start(f32[48]{0:T(128)} %param.13) | copy-start | bytes 580
  1.9 1.7 %copy-start.4 = (s32[48,2]{0,1:T(2,128)S(1)}, s32[48,2]{0,1:T(2,128)}, u32[]{:S(2)}) copy-start(s32[48,2]{0,1:T(2,128)} %param.15) | copy-start | bytes 1156
  2.8 25.3 %copy-start.2 = (f32[1,2,256,256]{3,2,1,0:T(8,128)S(1)}, f32[1,2,256,256]{3,2,1,0:T(8,128)}, u32[]{:S(2)}) copy-start(f32[1,2,256,256]{3,2,1,0:T(8,128)} %param.8) | copy-start | bytes 1572868
  2.8 5.9 %collective-permute-start = (f32[256,256]{1,0:T(8,128)S(1)}, f32[256,256]{1,0:T(8,128)S(1)}, u32[]{:S(2)}, u32[]{:S(2)}) collective-permute-start(f32[256,256]{1,0:T(8,128)S(1)} %convolution_select_fusion), channel_id=1, source_target_pairs={{0,8},{8,0},{16,24},{24,16},{1,9},{9,1},{17,25},{25,17},{2,10},{10... | collective-permute-start | bytes 786440 | tf_op jit(solution)/shard_map/ppermute | solution.py:23
  4.0 4.7 %collective-permute-start.10 = (f32[6]{0:T(128)S(1)}, f32[6]{0:T(128)S(1)}, u32[]{:S(2)}, u32[]{:S(2)}) collective-permute-start(f32[6]{0:T(128)S(1)} %get-tuple-element.12), channel_id=1, source_target_pairs={{0,2},{1,3},{2,0},{3,1},{4,6},{5,7},{6,4},{7,5},{8,10},{9,11},{10,... | collective-permute-start | bytes 80 | tf_op jit(solution)/shard_map/ppermute | solution.py:23
  6.6 12.0 %collective-permute-start.7 = (f32[384,256]{1,0:T(8,128)S(1)}, f32[384,256]{1,0:T(8,128)S(1)}, u32[]{:S(2)}, u32[]{:S(2)}) collective-permute-start(f32[384,256]{1,0:T(8,128)S(1)} %get-tuple-element.9), channel_id=1, source_target_pairs={{0,2},{1,3},{2,0},{3,1},{4,6},{5,7},{6,4},{7,5},{8,10},{9,11},{10,... | collective-permute-start | bytes 1179656 | tf_op jit(solution)/shard_map/ppermute | solution.py:23
  6.7 19.6 %collective-permute-start.11 = (f32[384,256]{1,0:T(8,128)S(1)}, f32[384,256]{1,0:T(8,128)S(1)}, u32[]{:S(2)}, u32[]{:S(2)}) collective-permute-start(f32[384,256]{1,0:T(8,128)S(1)} %get-tuple-element.10), channel_id=1, source_target_pairs={{0,2},{1,3},{2,0},{3,1},{4,6},{5,7},{6,4},{7,5},{8,10},{9,11},{10,... | collective-permute-start | bytes 1179656 | tf_op jit(solution)/shard_map/ppermute | solution.py:23
  9.0 18.8 %collective-permute-start.1 = (f32[256,256]{1,0:T(8,128)S(1)}, f32[256,256]{1,0:T(8,128)S(1)}, u32[]{:S(2)}, u32[]{:S(2)}) collective-permute-start(f32[256,256]{1,0:T(8,128)S(1)} %fusion.48), channel_id=1, source_target_pairs={{0,16},{8,24},{16,0},{24,8},{1,17},{9,25},{17,1},{25,9},{2,18},{10... | collective-permute-start | bytes 786440 | tf_op jit(solution)/shard_map/ppermute | solution.py:23
  18.6 26.8 %collective-permute-start.8 = (f32[384,256]{1,0:T(8,128)S(1)}, f32[384,256]{1,0:T(8,128)S(1)}, u32[]{:S(2)}, u32[]{:S(2)}) collective-permute-start(f32[384,256]{1,0:T(8,128)S(1)} %collective-permute-done.7), channel_id=1, source_target_pairs={{0,16},{8,24},{16,0},{24,8},{1,17},{9,25},{17,1},{25,9},{2,18},{10... | collective-permute-start | bytes 1179656 | tf_op jit(solution)/shard_map/ppermute | solution.py:23
  26.3 26.1 %collective-permute-start.12 = (f32[384,256]{1,0:T(8,128)S(1)}, f32[384,256]{1,0:T(8,128)S(1)}, u32[]{:S(2)}, u32[]{:S(2)}) collective-permute-start(f32[384,256]{1,0:T(8,128)S(1)} %collective-permute-done.11), channel_id=1, source_target_pairs={{0,16},{8,24},{16,0},{24,8},{1,17},{9,25},{17,1},{25,9},{2,18},{10... | collective-permute-start | bytes 1179656 | tf_op jit(solution)/shard_map/ppermute | solution.py:23
  28.1 1.4 %copy-start.1 = (f32[6,256,256]{2,1,0:T(8,128)S(1)}, f32[6,256,256]{2,1,0:T(8,128)}, u32[]{:S(2)}) copy-start(f32[6,256,256]{2,1,0:T(8,128)} %param.11) | copy-start | bytes 4718596
  29.6 1.4 %copy-start = (f32[6,256,256]{2,1,0:T(8,128)S(1)}, f32[6,256,256]{2,1,0:T(8,128)}, u32[]{:S(2)}) copy-start(f32[6,256,256]{2,1,0:T(8,128)} %param.12) | copy-start | bytes 4718596
  32.5 7.3 %collective-permute-start.2 = (f32[256,256]{1,0:T(8,128)S(1)}, f32[256,256]{1,0:T(8,128)S(1)}, u32[]{:S(2)}, u32[]{:S(2)}) collective-permute-start(f32[256,256]{1,0:T(8,128)S(1)} %convolution_bitcast_fusion.3), channel_id=1, source_target_pairs={{0,2},{1,3},{2,0},{3,1},{4,6},{5,7},{6,4},{7,5},{8,10},{9,11},{10,... | collective-permute-start | bytes 786440 | tf_op jit(solution)/shard_map/ppermute | solution.py:23
  41.3 6.9 %collective-permute-start.5 = (f32[128,256]{1,0:T(8,128)S(1)}, f32[128,256]{1,0:T(8,128)S(1)}, u32[]{:S(2)}, u32[]{:S(2)}) collective-permute-start(f32[128,256]{1,0:T(8,128)S(1)} %get-tuple-element.30), channel_id=1, source_target_pairs={{0,6},{1,7},{2,4},{3,5},{4,2},{5,3},{6,0},{7,1},{8,14},{9,15},{10,... | collective-permute-start | bytes 393224 | tf_op jit(solution)/shard_map/ppermute | solution.py:23
  43.9 6.0 %collective-permute-start.3 = (f32[128,256]{1,0:T(8,128)S(1)}, f32[128,256]{1,0:T(8,128)S(1)}, u32[]{:S(2)}, u32[]{:S(2)}) collective-permute-start(f32[128,256]{1,0:T(8,128)S(1)} %get-tuple-element.29), channel_id=1, source_target_pairs={{0,1},{1,0},{2,3},{3,2},{4,5},{5,4},{6,7},{7,6},{8,9},{9,8},{10,11... | collective-permute-start | bytes 393224 | tf_op jit(solution)/shard_map/ppermute | solution.py:23
  45.4 15.5 %collective-permute-start.9 = (f32[2,384,256]{2,1,0:T(8,128)S(1)}, f32[2,384,256]{2,1,0:T(8,128)S(1)}, u32[]{:S(2)}, u32[]{:S(2)}) collective-permute-start(f32[2,384,256]{2,1,0:T(8,128)S(1)} %pad_maximum_fusion.2), channel_id=1, source_target_pairs={{0,8},{8,0},{16,24},{24,16},{1,9},{9,1},{17,25},{25,17},{2,10},{10... | collective-permute-start | bytes 2359304 | tf_op jit(solution)/shard_map/ppermute | solution.py:23
  48.3 5.0 %collective-permute-start.6 = (f32[128,256]{1,0:T(8,128)S(1)}, f32[128,256]{1,0:T(8,128)S(1)}, u32[]{:S(2)}, u32[]{:S(2)}) collective-permute-start(f32[128,256]{1,0:T(8,128)S(1)} %add.91), channel_id=1, source_target_pairs={{0,1},{1,0},{2,3},{3,2},{4,5},{5,4},{6,7},{7,6},{8,9},{9,8},{10,11... | collective-permute-start | bytes 393224 | tf_op jit(solution)/shard_map/ppermute | solution.py:23
  49.9 6.8 %collective-permute-start.4 = (f32[128,256]{1,0:T(8,128)S(1)}, f32[128,256]{1,0:T(8,128)S(1)}, u32[]{:S(2)}, u32[]{:S(2)}) collective-permute-start(f32[128,256]{1,0:T(8,128)S(1)} %add.89), channel_id=1, source_target_pairs={{0,6},{1,7},{2,4},{3,5},{4,2},{5,3},{6,0},{7,1},{8,14},{9,15},{10,... | collective-permute-start | bytes 393224 | tf_op jit(solution)/shard_map/ppermute | solution.py:23
  52.5 8.1 %collective-permute-start.13 = (f32[2,384,256]{2,1,0:T(8,128)S(1)}, f32[2,384,256]{2,1,0:T(8,128)S(1)}, u32[]{:S(2)}, u32[]{:S(2)}) collective-permute-start(f32[2,384,256]{2,1,0:T(8,128)S(1)} %pad_maximum_fusion.3), channel_id=1, source_target_pairs={{0,8},{8,0},{16,24},{24,16},{1,9},{9,1},{17,25},{25,17},{2,10},{10... | collective-permute-start | bytes 2359304 | tf_op jit(solution)/shard_map/ppermute | solution.py:23
  63.0 6.9 %collective-permute-start.16 = (f32[128,256]{1,0:T(8,128)S(1)}, f32[128,256]{1,0:T(8,128)S(1)}, u32[]{:S(2)}, u32[]{:S(2)}) collective-permute-start(f32[128,256]{1,0:T(8,128)S(1)} %get-tuple-element.28), channel_id=1, source_target_pairs={{0,6},{1,7},{2,4},{3,5},{4,2},{5,3},{6,0},{7,1},{8,14},{9,15},{10,... | collective-permute-start | bytes 393224 | tf_op jit(solution)/shard_map/ppermute | solution.py:23
  65.6 5.7 %collective-permute-start.14 = (f32[128,256]{1,0:T(8,128)S(1)}, f32[128,256]{1,0:T(8,128)S(1)}, u32[]{:S(2)}, u32[]{:S(2)}) collective-permute-start(f32[128,256]{1,0:T(8,128)S(1)} %get-tuple-element.27), channel_id=1, source_target_pairs={{0,1},{1,0},{2,3},{3,2},{4,5},{5,4},{6,7},{7,6},{8,9},{9,8},{10,11... | collective-permute-start | bytes 393224 | tf_op jit(solution)/shard_map/ppermute | solution.py:23
  69.9 5.0 %collective-permute-start.17 = (f32[128,256]{1,0:T(8,128)S(1)}, f32[128,256]{1,0:T(8,128)S(1)}, u32[]{:S(2)}, u32[]{:S(2)}) collective-permute-start(f32[128,256]{1,0:T(8,128)S(1)} %add.96), channel_id=1, source_target_pairs={{0,1},{1,0},{2,3},{3,2},{4,5},{5,4},{6,7},{7,6},{8,9},{9,8},{10,11... | collective-permute-start | bytes 393224 | tf_op jit(solution)/shard_map/ppermute | solution.py:23
  71.4 6.9 %collective-permute-start.15 = (f32[128,256]{1,0:T(8,128)S(1)}, f32[128,256]{1,0:T(8,128)S(1)}, u32[]{:S(2)}, u32[]{:S(2)}) collective-permute-start(f32[128,256]{1,0:T(8,128)S(1)} %add.94), channel_id=1, source_target_pairs={{0,6},{1,7},{2,4},{3,5},{4,2},{5,3},{6,0},{7,1},{8,14},{9,15},{10,... | collective-permute-start | bytes 393224 | tf_op jit(solution)/shard_map/ppermute | solution.py:23
  81.3 7.3 %collective-permute-start.20 = (f32[128,256]{1,0:T(8,128)S(1)}, f32[128,256]{1,0:T(8,128)S(1)}, u32[]{:S(2)}, u32[]{:S(2)}) collective-permute-start(f32[128,256]{1,0:T(8,128)S(1)} %get-tuple-element.26), channel_id=1, source_target_pairs={{0,6},{1,7},{2,4},{3,5},{4,2},{5,3},{6,0},{7,1},{8,14},{9,15},{10,... | collective-permute-start | bytes 393224 | tf_op jit(solution)/shard_map/ppermute | solution.py:23
  83.2 6.1 %collective-permute-start.18 = (f32[128,256]{1,0:T(8,128)S(1)}, f32[128,256]{1,0:T(8,128)S(1)}, u32[]{:S(2)}, u32[]{:S(2)}) collective-permute-start(f32[128,256]{1,0:T(8,128)S(1)} %get-tuple-element.25), channel_id=1, source_target_pairs={{0,1},{1,0},{2,3},{3,2},{4,5},{5,4},{6,7},{7,6},{8,9},{9,8},{10,11... | collective-permute-start | bytes 393224 | tf_op jit(solution)/shard_map/ppermute | solution.py:23
  88.7 5.0 %collective-permute-start.21 = (f32[128,256]{1,0:T(8,128)S(1)}, f32[128,256]{1,0:T(8,128)S(1)}, u32[]{:S(2)}, u32[]{:S(2)}) collective-permute-start(f32[128,256]{1,0:T(8,128)S(1)} %add.101), channel_id=1, source_target_pairs={{0,1},{1,0},{2,3},{3,2},{4,5},{5,4},{6,7},{7,6},{8,9},{9,8},{10,11... | collective-permute-start | bytes 393224 | tf_op jit(solution)/shard_map/ppermute | solution.py:23
  89.4 6.9 %collective-permute-start.19 = (f32[128,256]{1,0:T(8,128)S(1)}, f32[128,256]{1,0:T(8,128)S(1)}, u32[]{:S(2)}, u32[]{:S(2)}) collective-permute-start(f32[128,256]{1,0:T(8,128)S(1)} %add.99), channel_id=1, source_target_pairs={{0,6},{1,7},{2,4},{3,5},{4,2},{5,3},{6,0},{7,1},{8,14},{9,15},{10,... | collective-permute-start | bytes 393224 | tf_op jit(solution)/shard_map/ppermute | solution.py:23
  100.4 6.9 %collective-permute-start.24 = (f32[128,256]{1,0:T(8,128)S(1)}, f32[128,256]{1,0:T(8,128)S(1)}, u32[]{:S(2)}, u32[]{:S(2)}) collective-permute-start(f32[128,256]{1,0:T(8,128)S(1)} %get-tuple-element.24), channel_id=1, source_target_pairs={{0,6},{1,7},{2,4},{3,5},{4,2},{5,3},{6,0},{7,1},{8,14},{9,15},{10,... | collective-permute-start | bytes 393224 | tf_op jit(solution)/shard_map/ppermute | solution.py:23
  103.9 5.9 %collective-permute-start.22 = (f32[128,256]{1,0:T(8,128)S(1)}, f32[128,256]{1,0:T(8,128)S(1)}, u32[]{:S(2)}, u32[]{:S(2)}) collective-permute-start(f32[128,256]{1,0:T(8,128)S(1)} %get-tuple-element.23), channel_id=1, source_target_pairs={{0,1},{1,0},{2,3},{3,2},{4,5},{5,4},{6,7},{7,6},{8,9},{9,8},{10,11... | collective-permute-start | bytes 393224 | tf_op jit(solution)/shard_map/ppermute | solution.py:23
  107.3 5.4 %collective-permute-start.25 = (f32[128,256]{1,0:T(8,128)S(1)}, f32[128,256]{1,0:T(8,128)S(1)}, u32[]{:S(2)}, u32[]{:S(2)}) collective-permute-start(f32[128,256]{1,0:T(8,128)S(1)} %add.108), channel_id=1, source_target_pairs={{0,1},{1,0},{2,3},{3,2},{4,5},{5,4},{6,7},{7,6},{8,9},{9,8},{10,11... | collective-permute-start | bytes 393224 | tf_op jit(solution)/shard_map/ppermute | solution.py:23
  109.8 6.9 %collective-permute-start.23 = (f32[128,256]{1,0:T(8,128)S(1)}, f32[128,256]{1,0:T(8,128)S(1)}, u32[]{:S(2)}, u32[]{:S(2)}) collective-permute-start(f32[128,256]{1,0:T(8,128)S(1)} %add.105), channel_id=1, source_target_pairs={{0,6},{1,7},{2,4},{3,5},{4,2},{5,3},{6,0},{7,1},{8,14},{9,15},{10,... | collective-permute-start | bytes 393224 | tf_op jit(solution)/shard_map/ppermute | solution.py:23
  116.8 5.0 %collective-permute-start.26 = (f32[128,256]{1,0:T(8,128)S(1)}, f32[128,256]{1,0:T(8,128)S(1)}, u32[]{:S(2)}, u32[]{:S(2)}) collective-permute-start(f32[128,256]{1,0:T(8,128)S(1)} %get-tuple-element.21), channel_id=1, source_target_pairs={{0,2},{1,3},{2,0},{3,1},{4,6},{5,7},{6,4},{7,5},{8,10},{9,11},{10,... | collective-permute-start | bytes 393224 | tf_op jit(solution)/shard_map/ppermute | solution.py:23
  118.3 5.0 %collective-permute-start.27 = (f32[128,256]{1,0:T(8,128)S(1)}, f32[128,256]{1,0:T(8,128)S(1)}, u32[]{:S(2)}, u32[]{:S(2)}) collective-permute-start(f32[128,256]{1,0:T(8,128)S(1)} %get-tuple-element.22), channel_id=1, source_target_pairs={{0,2},{1,3},{2,0},{3,1},{4,6},{5,7},{6,4},{7,5},{8,10},{9,11},{10,... | collective-permute-start | bytes 393224 | tf_op jit(solution)/shard_map/ppermute | solution.py:23

commit v3 on v2

--- a/solution.py
+++ b/solution.py
@@ -1,6 +1,7 @@
 import jax
 import jax.numpy as jnp
 from jax import lax
+from jax.experimental.layout import Layout, with_layout_constraint
 from jax.sharding import PartitionSpec as P
 
 ORDER = 4
@@ -84,7 +85,8 @@
     for i in range(len(masks)):
         from_upper = swap(upper, "term", masks[i])
         from_lower = swap(lower, "term", masks[-1 - i])
-        upper, lower = upper + from_upper, lower + from_lower
+        upper = upper + from_upper
+        lower = lower + from_lower
     return upper, lower
 
 
@@ -92,6 +94,7 @@
     lefted = contract("tij,jk->tik", lefts, tensor)
     if weights is not None:
         lefted = lax.optimization_barrier(lefted * weights[:, None, None])
+    lefted = with_layout_constraint(lefted, Layout(major_to_minor=(0, 1, 2)))
     return contract("tik,tkl->il", lefted, rights)
 
 
@@ -146,7 +149,7 @@
         return apply_terms(turned, left_edge, right_edge, weights)
 
     given = first(start_give, give_weight)
-    kept = first(start_keep, keep_weight)
+    kept = lax.optimization_barrier(first(start_keep, keep_weight))
     partial = kept + swap(given, "term", PAIR)
     current = jnp.concatenate(sum_groups(partial), axis=0) * (-TAYLOR_STEP)
     total = current
@@ -179,7 +182,7 @@
     ours, theirs = [], []
     for i, end in enumerate(ends):
         rows = end.shape[0]
-        end = so_far[i * rows : (i + 1) * rows] + end
+        end = lax.optimization_barrier(so_far[i * rows : (i + 1) * rows]) + end
         ours.append(end)
         theirs.append(swap(end, "term", PAIR))
     ours, theirs = jnp.concatenate(ours, axis=0), jnp.concatenate(theirs, axis=0)

time: 124 us -> 121 us (0.976)
  matrix products: 25.7 us -> 22.9 us
  waiting for transfers between devices: 50.4 us -> 48.3 us
    dot_general x20, matrix products: 22.4 us -> 19.6 us  [contract(): jnp.einsum(spec, left, right, precision=lax.Precision.HIGH, preferred_ele...]
    ppermute x28, waiting for transfers between devices: 50.4 us -> 48.3 us  [swap(): return lax.ppermute(value, axis, pairs)]
  transfers between devices with their start and end apart: 28 -> 28, of which waited for: 17 -> 17; matrix products, arithmetic and copies ran while one was open for 14% -> 12% of each run, Pallas kernels for 0% -> 0%
where the time goes in v3:
time: 121 us; the launch traced here: 120 us
  waiting for transfers between devices  48.3 us (40%)
  starting transfers between devices  43.3 us (36%)
  matrix products  22.9 us (19%)
  other arithmetic  2.5 us (2%)
  local copies, waits for them, and re-layouts  2.03 us (2%)
  between operations  1.27 us (1%)
    ppermute x28, waiting for transfers between devices, swap(): return lax.ppermute(value, axis, pairs)  48.3 us
    ppermute x28, starting transfers between devices, swap(): return lax.ppermute(value, axis, pairs)  43.3 us
    dot_general x20, matrix products, contract(): jnp.einsum(spec, left, right, precision=lax.Precision.HIGH, preferred_ele...  19.6 us
    dot_general x11, matrix products, product(): jnp.dot(left, right, precision=lax.Precision.HIGH, preferred_element_type...  3.32 us
  transfers between devices with their start and end apart: 28, of which 17 were waited for; matrix products, arithmetic and copies ran while one was open for 12% of the time, Pallas kernels for 0%

profile of v3, /device:TPU:0, one launch (start us, length us, event | category | flops | bytes accessed | tf_op | source)
XLA Modules:
  0.0 120.3 jit_solution(7677755716236234468)
XLA Ops:
  0.7 1.2 constant_dynamic-slice_fusion
  4.0 2.6 %collective-permute-start.10 = (f32[6]{0:T(128)S(1)}, f32[6]{0:T(128)S(1)}, u32[]{:S(2)}, u32[]{:S(2)}) collective-permute-start(f32[6]{0:T(128)S(1)} %get-tuple-element.12), channel_id=1, source_target_pairs={{0,2},{1,3},{2,0},{3,1},{4,6},{5,7},{6,4},{7,5},{8,10},{9,11},{10,... | collective-permute-start | bytes 80 | tf_op jit(solution)/shard_map/ppermute | solution.py:24
  6.7 1.9 %collective-permute-start.11 = (f32[384,256]{1,0:T(8,128)S(1)}, f32[384,256]{1,0:T(8,128)S(1)}, u32[]{:S(2)}, u32[]{:S(2)}) collective-permute-start(f32[384,256]{1,0:T(8,128)S(1)} %get-tuple-element.10), channel_id=1, source_target_pairs={{0,2},{1,3},{2,0},{3,1},{4,6},{5,7},{6,4},{7,5},{8,10},{9,11},{10,... | collective-permute-start | bytes 1179656 | tf_op jit(solution)/shard_map/ppermute | solution.py:24
  9.0 1.6 %collective-permute-start.1 = (f32[256,256]{1,0:T(8,128)S(1)}, f32[256,256]{1,0:T(8,128)S(1)}, u32[]{:S(2)}, u32[]{:S(2)}) collective-permute-start(f32[256,256]{1,0:T(8,128)S(1)} %fusion.47), channel_id=1, source_target_pairs={{0,16},{8,24},{16,0},{24,8},{1,17},{9,25},{17,1},{25,9},{2,18},{10... | collective-permute-start | bytes 786440 | tf_op jit(solution)/shard_map/ppermute | solution.py:24
  10.8 7.9 %collective-permute-done.7 = f32[384,256]{1,0:T(8,128)S(1)} collective-permute-done((f32[384,256]{1,0:T(8,128)S(1)}, f32[384,256]{1,0:T(8,128)S(1)}, u32[]{:S(2)}, u32[]{:S(2)}) %collective-permute-start.7) | collective-permute-done | bytes 393248 | tf_op jit(solution)/shard_map/ppermute | solution.py:24
  18.6 1.5 %collective-permute-start.8 = (f32[384,256]{1,0:T(8,128)S(1)}, f32[384,256]{1,0:T(8,128)S(1)}, u32[]{:S(2)}, u32[]{:S(2)}) collective-permute-start(f32[384,256]{1,0:T(8,128)S(1)} %collective-permute-done.7), channel_id=1, source_target_pairs={{0,16},{8,24},{16,0},{24,8},{1,17},{9,25},{17,1},{25,9},{2,18},{10... | collective-permute-start | bytes 1179656 | tf_op jit(solution)/shard_map/ppermute | solution.py:24
  20.1 6.1 %collective-permute-done.11 = f32[384,256]{1,0:T(8,128)S(1)} collective-permute-done((f32[384,256]{1,0:T(8,128)S(1)}, f32[384,256]{1,0:T(8,128)S(1)}, u32[]{:S(2)}, u32[]{:S(2)}) %collective-permute-start.11) | collective-permute-done | bytes 393248 | tf_op jit(solution)/shard_map/ppermute | solution.py:24
  26.3 1.5 %collective-permute-start.12 = (f32[384,256]{1,0:T(8,128)S(1)}, f32[384,256]{1,0:T(8,128)S(1)}, u32[]{:S(2)}, u32[]{:S(2)}) collective-permute-start(f32[384,256]{1,0:T(8,128)S(1)} %collective-permute-done.11), channel_id=1, source_target_pairs={{0,16},{8,24},{16,0},{24,8},{1,17},{9,25},{17,1},{25,9},{2,18},{10... | collective-permute-start | bytes 1179656 | tf_op jit(solution)/shard_map/ppermute | solution.py:24
  29.9 0.9 multiply_bitcast_fusion.1
  31.3 0.9 convolution_bitcast_fusion.3
  32.8 0.9 multiply_bitcast_fusion.2
  34.0 0.9 convolution_bitcast_fusion.5
  34.9 4.7 %collective-permute-done.2 = f32[256,256]{1,0:T(8,128)S(1)} collective-permute-done((f32[256,256]{1,0:T(8,128)S(1)}, f32[256,256]{1,0:T(8,128)S(1)}, u32[]{:S(2)}, u32[]{:S(2)}) %collective-permute-start.2) | collective-permute-done | bytes 262176 | tf_op jit(solution)/shard_map/ppermute | solution.py:24
  39.7 2.6 %collective-permute-start.5 = (f32[128,256]{1,0:T(8,128)S(1)}, f32[128,256]{1,0:T(8,128)S(1)}, u32[]{:S(2)}, u32[]{:S(2)}) collective-permute-start(f32[128,256]{1,0:T(8,128)S(1)} %get-tuple-element.30), channel_id=1, source_target_pairs={{0,6},{1,7},{2,4},{3,5},{4,2},{5,3},{6,0},{7,1},{8,14},{9,15},{10,... | collective-permute-start | bytes 393224 | tf_op jit(solution)/shard_map/ppermute | solution.py:24
  42.2 1.5 %collective-permute-start.3 = (f32[128,256]{1,0:T(8,128)S(1)}, f32[128,256]{1,0:T(8,128)S(1)}, u32[]{:S(2)}, u32[]{:S(2)}) collective-permute-start(f32[128,256]{1,0:T(8,128)S(1)} %get-tuple-element.29), channel_id=1, source_target_pairs={{0,1},{1,0},{2,3},{3,2},{4,5},{5,4},{6,7},{7,6},{8,9},{9,8},{10,11... | collective-permute-start | bytes 393224 | tf_op jit(solution)/shard_map/ppermute | solution.py:24
  43.8 2.8 %collective-permute-done.5 = f32[128,256]{1,0:T(8,128)S(1)} collective-permute-done((f32[128,256]{1,0:T(8,128)S(1)}, f32[128,256]{1,0:T(8,128)S(1)}, u32[]{:S(2)}, u32[]{:S(2)}) %collective-permute-start.5) | collective-permute-done | bytes 131104 | tf_op jit(solution)/shard_map/ppermute | solution.py:24
  46.6 1.6 %collective-permute-start.6 = (f32[128,256]{1,0:T(8,128)S(1)}, f32[128,256]{1,0:T(8,128)S(1)}, u32[]{:S(2)}, u32[]{:S(2)}) collective-permute-start(f32[128,256]{1,0:T(8,128)S(1)} %add.91), channel_id=1, source_target_pairs={{0,1},{1,0},{2,3},{3,2},{4,5},{5,4},{6,7},{7,6},{8,9},{9,8},{10,11... | collective-permute-start | bytes 393224 | tf_op jit(solution)/shard_map/ppermute | solution.py:24
  48.2 2.6 %collective-permute-start.4 = (f32[128,256]{1,0:T(8,128)S(1)}, f32[128,256]{1,0:T(8,128)S(1)}, u32[]{:S(2)}, u32[]{:S(2)}) collective-permute-start(f32[128,256]{1,0:T(8,128)S(1)} %add.89), channel_id=1, source_target_pairs={{0,6},{1,7},{2,4},{3,5},{4,2},{5,3},{6,0},{7,1},{8,14},{9,15},{10,... | collective-permute-start | bytes 393224 | tf_op jit(solution)/shard_map/ppermute | solution.py:24
  51.7 3.4 %collective-permute-done.4 = f32[128,256]{1,0:T(8,128)S(1)} collective-permute-done((f32[128,256]{1,0:T(8,128)S(1)}, f32[128,256]{1,0:T(8,128)S(1)}, u32[]{:S(2)}, u32[]{:S(2)}) %collective-permute-start.4) | collective-permute-done | bytes 131104 | tf_op jit(solution)/shard_map/ppermute | solution.py:24
  56.5 0.9 convolution_bitcast_fusion.1
  58.8 1.1 fusion.27
  59.9 2.6 %collective-permute-start.16 = (f32[128,256]{1,0:T(8,128)S(1)}, f32[128,256]{1,0:T(8,128)S(1)}, u32[]{:S(2)}, u32[]{:S(2)}) collective-permute-start(f32[128,256]{1,0:T(8,128)S(1)} %get-tuple-element.28), channel_id=1, source_target_pairs={{0,6},{1,7},{2,4},{3,5},{4,2},{5,3},{6,0},{7,1},{8,14},{9,15},{10,... | collective-permute-start | bytes 393224 | tf_op jit(solution)/shard_map/ppermute | solution.py:24
  63.1 2.7 %fusion.4 = f32[12,256,256]{2,1,0:T(8,128)S(1)} fusion(f32[6,256,256]{2,1,0:T(8,128)S(1)} %bitcast.143, f32[6,256,256]{2,1,0:T(8,128)S(1)} %copy-done.1, f32[256,256]{1,0:T(8,128)S(1)} %fusion.90), kind=kOutput, calls=%fused_computation.4 | convolution fusion | flops 1208745984 | bytes 6553600 | tf_op jit(solution)/shard_map/ij,tjk->tik/dot_general | solution.py:17
  65.8 1.1 collective-permute-done.16
  66.9 1.4 %collective-permute-start.17 = (f32[128,256]{1,0:T(8,128)S(1)}, f32[128,256]{1,0:T(8,128)S(1)}, u32[]{:S(2)}, u32[]{:S(2)}) collective-permute-start(f32[128,256]{1,0:T(8,128)S(1)} %add.96), channel_id=1, source_target_pairs={{0,1},{1,0},{2,3},{3,2},{4,5},{5,4},{6,7},{7,6},{8,9},{9,8},{10,11... | collective-permute-start | bytes 393224 | tf_op jit(solution)/shard_map/ppermute | solution.py:24
  68.3 1.8 %collective-permute-start.15 = (f32[128,256]{1,0:T(8,128)S(1)}, f32[128,256]{1,0:T(8,128)S(1)}, u32[]{:S(2)}, u32[]{:S(2)}) collective-permute-start(f32[128,256]{1,0:T(8,128)S(1)} %add.94), channel_id=1, source_target_pairs={{0,6},{1,7},{2,4},{3,5},{4,2},{5,3},{6,0},{7,1},{8,14},{9,15},{10,... | collective-permute-start | bytes 393224 | tf_op jit(solution)/shard_map/ppermute | solution.py:24
  70.1 1.4 %fusion = f32[12,256,256]{2,1,0:T(8,128)S(1)} fusion(f32[6,256,256]{2,1,0:T(8,128)S(1)} %bitcast.141, f32[6,256,256]{2,1,0:T(8,128)S(1)} %copy-done, f32[256,256]{1,0:T(8,128)S(1)} %fusion.89), kind=kOutput, calls=%fused_computation | convolution fusion | flops 1208745984 | bytes 6553600 | tf_op jit(solution)/shard_map/tij,jk->tik/dot_general | solution.py:17
  71.9 3.2 %collective-permute-done.15 = f32[128,256]{1,0:T(8,128)S(1)} collective-permute-done((f32[128,256]{1,0:T(8,128)S(1)}, f32[128,256]{1,0:T(8,128)S(1)}, u32[]{:S(2)}, u32[]{:S(2)}) %collective-permute-start.15) | collective-permute-done | bytes 131104 | tf_op jit(solution)/shard_map/ppermute | solution.py:24
  75.2 1.4 %fusion.14 = f32[12,256,256]{2,1,0:T(8,128)S(1)} fusion(f32[12,256,256]{2,1,0:T(8,128)S(1)} %fusion, f32[12]{0:T(128)S(1)} %pad_maximum_fusion.6, f32[128,256]{1,0:T(8,128)S(1)} %add.97, f32[128,256]{1,0:T(8,128)S(1)} %add.95), kind=kOutput, calls=%fused_computation.14 | convolution fusion | flops 1208877056 | bytes 6553648 | tf_op jit(solution)/shard_map/tij,jk->tik/dot_general | solution.py:17
  76.6 1.6 %fusion.18 = f32[256,256]{1,0:T(8,128)S(1)} fusion(f32[12,256,256]{2,1,0:T(8,128)S(1)} %fusion.14, f32[12,256,256]{2,1,0:T(8,128)S(1)} %fusion.4), kind=kOutput, calls=%fused_computation.34 | convolution fusion | flops 1207959552 | bytes 6553600 | tf_op jit(solution)/shard_map/tik,tkl->il/dot_general | solution.py:17
  78.3 1.9 %collective-permute-start.20 = (f32[128,256]{1,0:T(8,128)S(1)}, f32[128,256]{1,0:T(8,128)S(1)}, u32[]{:S(2)}, u32[]{:S(2)}) collective-permute-start(f32[128,256]{1,0:T(8,128)S(1)} %get-tuple-element.26), channel_id=1, source_target_pairs={{0,6},{1,7},{2,4},{3,5},{4,2},{5,3},{6,0},{7,1},{8,14},{9,15},{10,... | collective-permute-start | bytes 393224 | tf_op jit(solution)/shard_map/ppermute | solution.py:24
  80.2 1.9 %collective-permute-start.18 = (f32[128,256]{1,0:T(8,128)S(1)}, f32[128,256]{1,0:T(8,128)S(1)}, u32[]{:S(2)}, u32[]{:S(2)}) collective-permute-start(f32[128,256]{1,0:T(8,128)S(1)} %get-tuple-element.25), channel_id=1, source_target_pairs={{0,1},{1,0},{2,3},{3,2},{4,5},{5,4},{6,7},{7,6},{8,9},{9,8},{10,11... | collective-permute-start | bytes 393224 | tf_op jit(solution)/shard_map/ppermute | solution.py:24
  82.1 3.5 %collective-permute-done.20 = f32[128,256]{1,0:T(8,128)S(1)} collective-permute-done((f32[128,256]{1,0:T(8,128)S(1)}, f32[128,256]{1,0:T(8,128)S(1)}, u32[]{:S(2)}, u32[]{:S(2)}) %collective-permute-start.20) | collective-permute-done | bytes 131104 | tf_op jit(solution)/shard_map/ppermute | solution.py:24
  86.3 2.7 %collective-permute-start.19 = (f32[128,256]{1,0:T(8,128)S(1)}, f32[128,256]{1,0:T(8,128)S(1)}, u32[]{:S(2)}, u32[]{:S(2)}) collective-permute-start(f32[128,256]{1,0:T(8,128)S(1)} %add.99), channel_id=1, source_target_pairs={{0,6},{1,7},{2,4},{3,5},{4,2},{5,3},{6,0},{7,1},{8,14},{9,15},{10,... | collective-permute-start | bytes 393224 | tf_op jit(solution)/shard_map/ppermute | solution.py:24
  89.0 1.6 %collective-permute-done.21 = f32[128,256]{1,0:T(8,128)S(1)} collective-permute-done((f32[128,256]{1,0:T(8,128)S(1)}, f32[128,256]{1,0:T(8,128)S(1)}, u32[]{:S(2)}, u32[]{:S(2)}) %collective-permute-start.21) | collective-permute-done | bytes 131104 | tf_op jit(solution)/shard_map/ppermute | solution.py:24
  90.7 2.5 %collective-permute-done.19 = f32[128,256]{1,0:T(8,128)S(1)} collective-permute-done((f32[128,256]{1,0:T(8,128)S(1)}, f32[128,256]{1,0:T(8,128)S(1)}, u32[]{:S(2)}, u32[]{:S(2)}) %collective-permute-start.19) | collective-permute-done | bytes 131104 | tf_op jit(solution)/shard_map/ppermute | solution.py:24
  93.7 1.4 %fusion.12 = f32[12,256,256]{2,1,0:T(8,128)S(1)} fusion(f32[12,256,256]{2,1,0:T(8,128)S(1)} %fusion, f32[12]{0:T(128)S(1)} %pad_maximum_fusion.6, f32[128,256]{1,0:T(8,128)S(1)} %add.102, f32[128,256]{1,0:T(8,128)S(1)} %add.100), kind=kOutput, calls=%fused_computation.12 | convolution fusion | flops 1208877056 | bytes 6553648 | tf_op jit(solution)/shard_map/tij,jk->tik/dot_general | solution.py:17
  95.1 1.6 %fusion.24 = f32[256,256]{1,0:T(8,128)S(1)} fusion(f32[12,256,256]{2,1,0:T(8,128)S(1)} %fusion.12, f32[12,256,256]{2,1,0:T(8,128)S(1)} %fusion.4), kind=kOutput, calls=%fused_computation.36 | convolution fusion | flops 1208025088 | bytes 6553600 | tf_op jit(solution)/shard_map/tik,tkl->il/dot_general | solution.py:17
  97.5 3.4 %collective-permute-start.24 = (f32[128,256]{1,0:T(8,128)S(1)}, f32[128,256]{1,0:T(8,128)S(1)}, u32[]{:S(2)}, u32[]{:S(2)}) collective-permute-start(f32[128,256]{1,0:T(8,128)S(1)} %get-tuple-element.22), channel_id=1, source_target_pairs={{0,6},{1,7},{2,4},{3,5},{4,2},{5,3},{6,0},{7,1},{8,14},{9,15},{10,... | collective-permute-start | bytes 393224 | tf_op jit(solution)/shard_map/ppermute | solution.py:24
  101.6 3.0 %collective-permute-done.24 = f32[128,256]{1,0:T(8,128)S(1)} collective-permute-done((f32[128,256]{1,0:T(8,128)S(1)}, f32[128,256]{1,0:T(8,128)S(1)}, u32[]{:S(2)}, u32[]{:S(2)}) %collective-permute-start.24) | collective-permute-done | bytes 131104 | tf_op jit(solution)/shard_map/ppermute | solution.py:24
  104.7 2.7 %collective-permute-start.25 = (f32[128,256]{1,0:T(8,128)S(1)}, f32[128,256]{1,0:T(8,128)S(1)}, u32[]{:S(2)}, u32[]{:S(2)}) collective-permute-start(f32[128,256]{1,0:T(8,128)S(1)} %add.108), channel_id=1, source_target_pairs={{0,1},{1,0},{2,3},{3,2},{4,5},{5,4},{6,7},{7,6},{8,9},{9,8},{10,11... | collective-permute-start | bytes 393224 | tf_op jit(solution)/shard_map/ppermute | solution.py:24
  107.4 1.8 %collective-permute-start.23 = (f32[128,256]{1,0:T(8,128)S(1)}, f32[128,256]{1,0:T(8,128)S(1)}, u32[]{:S(2)}, u32[]{:S(2)}) collective-permute-start(f32[128,256]{1,0:T(8,128)S(1)} %add.105), channel_id=1, source_target_pairs={{0,6},{1,7},{2,4},{3,5},{4,2},{5,3},{6,0},{7,1},{8,14},{9,15},{10,... | collective-permute-start | bytes 393224 | tf_op jit(solution)/shard_map/ppermute | solution.py:24
  109.2 1.1 collective-permute-done.25
  110.4 1.8 %collective-permute-start.27 = (f32[128,256]{1,0:T(8,128)S(1)}, f32[128,256]{1,0:T(8,128)S(1)}, u32[]{:S(2)}, u32[]{:S(2)}) collective-permute-start(f32[128,256]{1,0:T(8,128)S(1)} %add_add_fusion), channel_id=1, source_target_pairs={{0,2},{1,3},{2,0},{3,1},{4,6},{5,7},{6,4},{7,5},{8,10},{9,11},{10,... | collective-permute-start | bytes 393224 | tf_op jit(solution)/shard_map/ppermute | solution.py:24
  112.1 2.3 %collective-permute-done.23 = f32[128,256]{1,0:T(8,128)S(1)} collective-permute-done((f32[128,256]{1,0:T(8,128)S(1)}, f32[128,256]{1,0:T(8,128)S(1)}, u32[]{:S(2)}, u32[]{:S(2)}) %collective-permute-start.23) | collective-permute-done | bytes 131104 | tf_op jit(solution)/shard_map/ppermute | solution.py:24
  114.4 1.0 collective-permute-start.26
  115.8 3.7 %collective-permute-done.26 = f32[128,256]{1,0:T(8,128)S(1)} collective-permute-done((f32[128,256]{1,0:T(8,128)S(1)}, f32[128,256]{1,0:T(8,128)S(1)}, u32[]{:S(2)}, u32[]{:S(2)}) %collective-permute-start.26) | collective-permute-done | bytes 131104 | tf_op jit(solution)/shard_map/ppermute | solution.py:24
  119.5 0.8 maximum_bitcast_fusion
  (94 shorter events, 14.1 us)
Async XLA Ops:
  0.0 2.0 %copy-start.3 = (f32[4,256,256]{2,1,0:T(8,128)S(1)}, f32[4,256,256]{2,1,0:T(8,128)}, u32[]{:S(2)}) copy-start(f32[4,256,256]{2,1,0:T(8,128)} %param.9) | copy-start | bytes 3145732
  1.9 1.4 %copy-start.5 = (s32[6]{0:T(128)S(1)}, s32[6]{0:T(128)}, u32[]{:S(2)}) copy-start(s32[6]{0:T(128)} %param.14) | copy-start | bytes 76
  1.9 1.5 %copy-start.6 = (f32[48]{0:T(128)S(1)}, f32[48]{0:T(128)}, u32[]{:S(2)}) copy-start(f32[48]{0:T(128)} %param.13) | copy-start | bytes 580
  1.9 1.7 %copy-start.4 = (s32[48,2]{0,1:T(2,128)S(1)}, s32[48,2]{0,1:T(2,128)}, u32[]{:S(2)}) copy-start(s32[48,2]{0,1:T(2,128)} %param.15) | copy-start | bytes 1156
  2.8 5.9 %collective-permute-start = (f32[256,256]{1,0:T(8,128)S(1)}, f32[256,256]{1,0:T(8,128)S(1)}, u32[]{:S(2)}, u32[]{:S(2)}) collective-permute-start(f32[256,256]{1,0:T(8,128)S(1)} %convolution_select_fusion), channel_id=1, source_target_pairs={{0,8},{8,0},{16,24},{24,16},{1,9},{9,1},{17,25},{25,17},{2,10},{10... | collective-permute-start | bytes 786440 | tf_op jit(solution)/shard_map/ppermute | solution.py:24
  4.0 4.7 %collective-permute-start.10 = (f32[6]{0:T(128)S(1)}, f32[6]{0:T(128)S(1)}, u32[]{:S(2)}, u32[]{:S(2)}) collective-permute-start(f32[6]{0:T(128)S(1)} %get-tuple-element.12), channel_id=1, source_target_pairs={{0,2},{1,3},{2,0},{3,1},{4,6},{5,7},{6,4},{7,5},{8,10},{9,11},{10,... | collective-permute-start | bytes 80 | tf_op jit(solution)/shard_map/ppermute | solution.py:24
  6.6 12.0 %collective-permute-start.7 = (f32[384,256]{1,0:T(8,128)S(1)}, f32[384,256]{1,0:T(8,128)S(1)}, u32[]{:S(2)}, u32[]{:S(2)}) collective-permute-start(f32[384,256]{1,0:T(8,128)S(1)} %get-tuple-element.9), channel_id=1, source_target_pairs={{0,2},{1,3},{2,0},{3,1},{4,6},{5,7},{6,4},{7,5},{8,10},{9,11},{10,... | collective-permute-start | bytes 1179656 | tf_op jit(solution)/shard_map/ppermute | solution.py:24
  6.7 19.6 %collective-permute-start.11 = (f32[384,256]{1,0:T(8,128)S(1)}, f32[384,256]{1,0:T(8,128)S(1)}, u32[]{:S(2)}, u32[]{:S(2)}) collective-permute-start(f32[384,256]{1,0:T(8,128)S(1)} %get-tuple-element.10), channel_id=1, source_target_pairs={{0,2},{1,3},{2,0},{3,1},{4,6},{5,7},{6,4},{7,5},{8,10},{9,11},{10,... | collective-permute-start | bytes 1179656 | tf_op jit(solution)/shard_map/ppermute | solution.py:24
  8.7 19.8 %copy-start.2 = (f32[1,2,256,256]{3,2,1,0:T(8,128)S(1)}, f32[1,2,256,256]{3,2,1,0:T(8,128)}, u32[]{:S(2)}) copy-start(f32[1,2,256,256]{3,2,1,0:T(8,128)} %param.8) | copy-start | bytes 1572868
  9.0 18.8 %collective-permute-start.1 = (f32[256,256]{1,0:T(8,128)S(1)}, f32[256,256]{1,0:T(8,128)S(1)}, u32[]{:S(2)}, u32[]{:S(2)}) collective-permute-start(f32[256,256]{1,0:T(8,128)S(1)} %fusion.47), channel_id=1, source_target_pairs={{0,16},{8,24},{16,0},{24,8},{1,17},{9,25},{17,1},{25,9},{2,18},{10... | collective-permute-start | bytes 786440 | tf_op jit(solution)/shard_map/ppermute | solution.py:24
  18.6 25.1 %collective-permute-start.8 = (f32[384,256]{1,0:T(8,128)S(1)}, f32[384,256]{1,0:T(8,128)S(1)}, u32[]{:S(2)}, u32[]{:S(2)}) collective-permute-start(f32[384,256]{1,0:T(8,128)S(1)} %collective-permute-done.7), channel_id=1, source_target_pairs={{0,16},{8,24},{16,0},{24,8},{1,17},{9,25},{17,1},{25,9},{2,18},{10... | collective-permute-start | bytes 1179656 | tf_op jit(solution)/shard_map/ppermute | solution.py:24
  26.3 24.5 %collective-permute-start.12 = (f32[384,256]{1,0:T(8,128)S(1)}, f32[384,256]{1,0:T(8,128)S(1)}, u32[]{:S(2)}, u32[]{:S(2)}) collective-permute-start(f32[384,256]{1,0:T(8,128)S(1)} %collective-permute-done.11), channel_id=1, source_target_pairs={{0,16},{8,24},{16,0},{24,8},{1,17},{9,25},{17,1},{25,9},{2,18},{10... | collective-permute-start | bytes 1179656 | tf_op jit(solution)/shard_map/ppermute | solution.py:24
  28.5 1.4 %copy-start = (f32[6,256,256]{2,1,0:T(8,128)S(1)}, f32[6,256,256]{2,1,0:T(8,128)}, u32[]{:S(2)}) copy-start(f32[6,256,256]{2,1,0:T(8,128)} %param.11) | copy-start | bytes 4718596
  29.9 1.4 %copy-start.1 = (f32[6,256,256]{2,1,0:T(8,128)S(1)}, f32[6,256,256]{2,1,0:T(8,128)}, u32[]{:S(2)}) copy-start(f32[6,256,256]{2,1,0:T(8,128)} %param.12) | copy-start | bytes 4718596
  32.2 7.3 %collective-permute-start.2 = (f32[256,256]{1,0:T(8,128)S(1)}, f32[256,256]{1,0:T(8,128)S(1)}, u32[]{:S(2)}, u32[]{:S(2)}) collective-permute-start(f32[256,256]{1,0:T(8,128)S(1)} %convolution_bitcast_fusion.3), channel_id=1, source_target_pairs={{0,2},{1,3},{2,0},{3,1},{4,6},{5,7},{6,4},{7,5},{8,10},{9,11},{10,... | collective-permute-start | bytes 786440 | tf_op jit(solution)/shard_map/ppermute | solution.py:24
  39.7 6.9 %collective-permute-start.5 = (f32[128,256]{1,0:T(8,128)S(1)}, f32[128,256]{1,0:T(8,128)S(1)}, u32[]{:S(2)}, u32[]{:S(2)}) collective-permute-start(f32[128,256]{1,0:T(8,128)S(1)} %get-tuple-element.30), channel_id=1, source_target_pairs={{0,6},{1,7},{2,4},{3,5},{4,2},{5,3},{6,0},{7,1},{8,14},{9,15},{10,... | collective-permute-start | bytes 393224 | tf_op jit(solution)/shard_map/ppermute | solution.py:24
  42.2 6.0 %collective-permute-start.3 = (f32[128,256]{1,0:T(8,128)S(1)}, f32[128,256]{1,0:T(8,128)S(1)}, u32[]{:S(2)}, u32[]{:S(2)}) collective-permute-start(f32[128,256]{1,0:T(8,128)S(1)} %get-tuple-element.29), channel_id=1, source_target_pairs={{0,1},{1,0},{2,3},{3,2},{4,5},{5,4},{6,7},{7,6},{8,9},{9,8},{10,11... | collective-permute-start | bytes 393224 | tf_op jit(solution)/shard_map/ppermute | solution.py:24
  43.8 14.0 %collective-permute-start.9 = (f32[2,384,256]{2,1,0:T(8,128)S(1)}, f32[2,384,256]{2,1,0:T(8,128)S(1)}, u32[]{:S(2)}, u32[]{:S(2)}) collective-permute-start(f32[2,384,256]{2,1,0:T(8,128)S(1)} %pad_maximum_fusion.2), channel_id=1, source_target_pairs={{0,8},{8,0},{16,24},{24,16},{1,9},{9,1},{17,25},{25,17},{2,10},{10... | collective-permute-start | bytes 2359304 | tf_op jit(solution)/shard_map/ppermute | solution.py:24
  46.6 5.0 %collective-permute-start.6 = (f32[128,256]{1,0:T(8,128)S(1)}, f32[128,256]{1,0:T(8,128)S(1)}, u32[]{:S(2)}, u32[]{:S(2)}) collective-permute-start(f32[128,256]{1,0:T(8,128)S(1)} %add.91), channel_id=1, source_target_pairs={{0,1},{1,0},{2,3},{3,2},{4,5},{5,4},{6,7},{7,6},{8,9},{9,8},{10,11... | collective-permute-start | bytes 393224 | tf_op jit(solution)/shard_map/ppermute | solution.py:24
  48.2 6.8 %collective-permute-start.4 = (f32[128,256]{1,0:T(8,128)S(1)}, f32[128,256]{1,0:T(8,128)S(1)}, u32[]{:S(2)}, u32[]{:S(2)}) collective-permute-start(f32[128,256]{1,0:T(8,128)S(1)} %add.89), channel_id=1, source_target_pairs={{0,6},{1,7},{2,4},{3,5},{4,2},{5,3},{6,0},{7,1},{8,14},{9,15},{10,... | collective-permute-start | bytes 393224 | tf_op jit(solution)/shard_map/ppermute | solution.py:24
  50.8 6.6 %collective-permute-start.13 = (f32[2,384,256]{2,1,0:T(8,128)S(1)}, f32[2,384,256]{2,1,0:T(8,128)S(1)}, u32[]{:S(2)}, u32[]{:S(2)}) collective-permute-start(f32[2,384,256]{2,1,0:T(8,128)S(1)} %pad_maximum_fusion.3), channel_id=1, source_target_pairs={{0,8},{8,0},{16,24},{24,16},{1,9},{9,1},{17,25},{25,17},{2,10},{10... | collective-permute-start | bytes 2359304 | tf_op jit(solution)/shard_map/ppermute | solution.py:24
  59.9 6.9 %collective-permute-start.16 = (f32[128,256]{1,0:T(8,128)S(1)}, f32[128,256]{1,0:T(8,128)S(1)}, u32[]{:S(2)}, u32[]{:S(2)}) collective-permute-start(f32[128,256]{1,0:T(8,128)S(1)} %get-tuple-element.28), channel_id=1, source_target_pairs={{0,6},{1,7},{2,4},{3,5},{4,2},{5,3},{6,0},{7,1},{8,14},{9,15},{10,... | collective-permute-start | bytes 393224 | tf_op jit(solution)/shard_map/ppermute | solution.py:24
  62.6 5.7 %collective-permute-start.14 = (f32[128,256]{1,0:T(8,128)S(1)}, f32[128,256]{1,0:T(8,128)S(1)}, u32[]{:S(2)}, u32[]{:S(2)}) collective-permute-start(f32[128,256]{1,0:T(8,128)S(1)} %get-tuple-element.27), channel_id=1, source_target_pairs={{0,1},{1,0},{2,3},{3,2},{4,5},{5,4},{6,7},{7,6},{8,9},{9,8},{10,11... | collective-permute-start | bytes 393224 | tf_op jit(solution)/shard_map/ppermute | solution.py:24
  66.9 5.0 %collective-permute-start.17 = (f32[128,256]{1,0:T(8,128)S(1)}, f32[128,256]{1,0:T(8,128)S(1)}, u32[]{:S(2)}, u32[]{:S(2)}) collective-permute-start(f32[128,256]{1,0:T(8,128)S(1)} %add.96), channel_id=1, source_target_pairs={{0,1},{1,0},{2,3},{3,2},{4,5},{5,4},{6,7},{7,6},{8,9},{9,8},{10,11... | collective-permute-start | bytes 393224 | tf_op jit(solution)/shard_map/ppermute | solution.py:24
  68.3 6.9 %collective-permute-start.15 = (f32[128,256]{1,0:T(8,128)S(1)}, f32[128,256]{1,0:T(8,128)S(1)}, u32[]{:S(2)}, u32[]{:S(2)}) collective-permute-start(f32[128,256]{1,0:T(8,128)S(1)} %add.94), channel_id=1, source_target_pairs={{0,6},{1,7},{2,4},{3,5},{4,2},{5,3},{6,0},{7,1},{8,14},{9,15},{10,... | collective-permute-start | bytes 393224 | tf_op jit(solution)/shard_map/ppermute | solution.py:24
  78.3 7.3 %collective-permute-start.20 = (f32[128,256]{1,0:T(8,128)S(1)}, f32[128,256]{1,0:T(8,128)S(1)}, u32[]{:S(2)}, u32[]{:S(2)}) collective-permute-start(f32[128,256]{1,0:T(8,128)S(1)} %get-tuple-element.26), channel_id=1, source_target_pairs={{0,6},{1,7},{2,4},{3,5},{4,2},{5,3},{6,0},{7,1},{8,14},{9,15},{10,... | collective-permute-start | bytes 393224 | tf_op jit(solution)/shard_map/ppermute | solution.py:24
  80.2 6.1 %collective-permute-start.18 = (f32[128,256]{1,0:T(8,128)S(1)}, f32[128,256]{1,0:T(8,128)S(1)}, u32[]{:S(2)}, u32[]{:S(2)}) collective-permute-start(f32[128,256]{1,0:T(8,128)S(1)} %get-tuple-element.25), channel_id=1, source_target_pairs={{0,1},{1,0},{2,3},{3,2},{4,5},{5,4},{6,7},{7,6},{8,9},{9,8},{10,11... | collective-permute-start | bytes 393224 | tf_op jit(solution)/shard_map/ppermute | solution.py:24
  85.6 5.0 %collective-permute-start.21 = (f32[128,256]{1,0:T(8,128)S(1)}, f32[128,256]{1,0:T(8,128)S(1)}, u32[]{:S(2)}, u32[]{:S(2)}) collective-permute-start(f32[128,256]{1,0:T(8,128)S(1)} %add.101), channel_id=1, source_target_pairs={{0,1},{1,0},{2,3},{3,2},{4,5},{5,4},{6,7},{7,6},{8,9},{9,8},{10,11... | collective-permute-start | bytes 393224 | tf_op jit(solution)/shard_map/ppermute | solution.py:24
  86.3 6.9 %collective-permute-start.19 = (f32[128,256]{1,0:T(8,128)S(1)}, f32[128,256]{1,0:T(8,128)S(1)}, u32[]{:S(2)}, u32[]{:S(2)}) collective-permute-start(f32[128,256]{1,0:T(8,128)S(1)} %add.99), channel_id=1, source_target_pairs={{0,6},{1,7},{2,4},{3,5},{4,2},{5,3},{6,0},{7,1},{8,14},{9,15},{10,... | collective-permute-start | bytes 393224 | tf_op jit(solution)/shard_map/ppermute | solution.py:24
  97.5 7.2 %collective-permute-start.24 = (f32[128,256]{1,0:T(8,128)S(1)}, f32[128,256]{1,0:T(8,128)S(1)}, u32[]{:S(2)}, u32[]{:S(2)}) collective-permute-start(f32[128,256]{1,0:T(8,128)S(1)} %get-tuple-element.22), channel_id=1, source_target_pairs={{0,6},{1,7},{2,4},{3,5},{4,2},{5,3},{6,0},{7,1},{8,14},{9,15},{10,... | collective-permute-start | bytes 393224 | tf_op jit(solution)/shard_map/ppermute | solution.py:24
  100.8 6.6 %collective-permute-start.22 = (f32[128,256]{1,0:T(8,128)S(1)}, f32[128,256]{1,0:T(8,128)S(1)}, u32[]{:S(2)}, u32[]{:S(2)}) collective-permute-start(f32[128,256]{1,0:T(8,128)S(1)} %get-tuple-element.21), channel_id=1, source_target_pairs={{0,1},{1,0},{2,3},{3,2},{4,5},{5,4},{6,7},{7,6},{8,9},{9,8},{10,11... | collective-permute-start | bytes 393224 | tf_op jit(solution)/shard_map/ppermute | solution.py:24
  104.7 5.7 %collective-permute-start.25 = (f32[128,256]{1,0:T(8,128)S(1)}, f32[128,256]{1,0:T(8,128)S(1)}, u32[]{:S(2)}, u32[]{:S(2)}) collective-permute-start(f32[128,256]{1,0:T(8,128)S(1)} %add.108), channel_id=1, source_target_pairs={{0,1},{1,0},{2,3},{3,2},{4,5},{5,4},{6,7},{7,6},{8,9},{9,8},{10,11... | collective-permute-start | bytes 393224 | tf_op jit(solution)/shard_map/ppermute | solution.py:24
  107.4 7.0 %collective-permute-start.23 = (f32[128,256]{1,0:T(8,128)S(1)}, f32[128,256]{1,0:T(8,128)S(1)}, u32[]{:S(2)}, u32[]{:S(2)}) collective-permute-start(f32[128,256]{1,0:T(8,128)S(1)} %add.105), channel_id=1, source_target_pairs={{0,6},{1,7},{2,4},{3,5},{4,2},{5,3},{6,0},{7,1},{8,14},{9,15},{10,... | collective-permute-start | bytes 393224 | tf_op jit(solution)/shard_map/ppermute | solution.py:24
  110.4 5.4 %collective-permute-start.27 = (f32[128,256]{1,0:T(8,128)S(1)}, f32[128,256]{1,0:T(8,128)S(1)}, u32[]{:S(2)}, u32[]{:S(2)}) collective-permute-start(f32[128,256]{1,0:T(8,128)S(1)} %add_add_fusion), channel_id=1, source_target_pairs={{0,2},{1,3},{2,0},{3,1},{4,6},{5,7},{6,4},{7,5},{8,10},{9,11},{10,... | collective-permute-start | bytes 393224 | tf_op jit(solution)/shard_map/ppermute | solution.py:24
  114.4 5.0 %collective-permute-start.26 = (f32[128,256]{1,0:T(8,128)S(1)}, f32[128,256]{1,0:T(8,128)S(1)}, u32[]{:S(2)}, u32[]{:S(2)}) collective-permute-start(f32[128,256]{1,0:T(8,128)S(1)} %add_add_fusion.1), channel_id=1, source_target_pairs={{0,2},{1,3},{2,0},{3,1},{4,6},{5,7},{6,4},{7,5},{8,10},{9,11},{10,... | collective-permute-start | bytes 393224 | tf_op jit(solution)/shard_map/ppermute | solution.py:24
